TPU v7x, 32 devices: a whole 2x2x4 slice. The times are simulated.
32 devices in a mesh: dp: 2 (over x), segment: 4 (over y, core), space: 4 (over z).
Axes of the slice: x: 2, y: 2, z: 4, core: 2. Of those that a mesh axis runs over, the one named last changes fastest.
Arguments:
- features: bfloat16 [2, 4, 32, 24, 6, 256], P('dp', 'segment', None, 'space'), may hold values from -6 to 6
- out_grad: bfloat16 [2, 4, 64, 12, 3, 128], P('dp', 'segment', None, 'space'), may hold values from -6 to 6
- weight_mean: float32 [4, 27, 2048], P('segment'), may hold values from -0.21875 to 0.21875
- weight_noise: float32 [4, 27, 2048], P('segment'), may hold values from -4 to 4
- precision: float32 [4, 27, 2048], P('segment'), may hold values from 0.5 to 4
Outputs:
- act_in: bfloat16 [2, 4, 64, 12, 3, 128], P('dp', 'segment', None, 'space')
- grad_in: bfloat16 [2, 4, 32, 24, 6, 256], P('dp', 'segment', None, 'space')
- mean_next: float32 [4, 27, 2048], P('segment')
- precision_next: float32 [4, 27, 2048], P('segment')
All inputs are finite; a program needn't handle non-finite values.
Results may differ from a plain program's by a relative error of at most 0.007.
Values may be sent and summed in bfloat16 or wider, within the bound.
No kernel may reach another device: no remote copies, remote signals or barrier semaphores. Data moves between devices by JAX's collectives and lax.ppermute only.
A program may use at most 64 MiB of HBM per device.

v0:
```python
import math

import jax
import jax.numpy as jnp
from jax import lax
from jax.sharding import PartitionSpec as P

CONV_LAYOUT = ("NCDHW", "OIDHW", "NCDHW")


def passed_along(block, axis, distance):
    devices = range(lax.axis_size(axis))
    route = [(i - distance, i) for i in devices if i - distance in devices]
    return lax.ppermute(block, axis, route)


def noisy_weights(weight_mean, weight_noise, precision, cout, cin):
    noisy = weight_mean + weight_noise * lax.rsqrt(2000.0 * (precision + 0.1))
    kernel = noisy.astype(jnp.bfloat16).reshape(3, 3, 3, cout, cin)
    return jnp.transpose(kernel, (3, 4, 0, 1, 2))


def forward_conv(padded, kernel):
    return lax.conv_general_dilated(
        padded[None],
        kernel,
        (2, 2, 2),
        "VALID",
        dimension_numbers=CONV_LAYOUT,
        preferred_element_type=jnp.float32,
    )[0]


def input_conv(pre_grad, kernel):
    flipped = jnp.transpose(kernel[:, :, ::-1, ::-1, ::-1], (1, 0, 2, 3, 4))
    return lax.conv_general_dilated(
        pre_grad[None],
        flipped,
        (1, 1, 1),
        ((2, 2), (2, 2), (2, 2)),
        lhs_dilation=(2, 2, 2),
        dimension_numbers=CONV_LAYOUT,
        preferred_element_type=jnp.float32,
    )[0]


def weight_conv(padded, pre_grad):
    grads = lax.conv_general_dilated(
        padded[:, None],
        pre_grad[:, None],
        (1, 1, 1),
        "VALID",
        rhs_dilation=(2, 2, 2),
        dimension_numbers=CONV_LAYOUT,
        preferred_element_type=jnp.float32,
    )
    return jnp.transpose(grads, (2, 3, 4, 1, 0)).reshape(27, -1)


def input_grad(pre_grad, kernel):
    spread_grad = input_conv(pre_grad, kernel)
    rim_plane = passed_along(spread_grad[:, 0, 1:, 1:], "space", -1)
    interior = spread_grad[:, 1:, 1:, 1:]
    interior = jnp.concatenate([interior[:, :-1], interior[:, -1:] + rim_plane[:, None]], axis=1)
    return interior.astype(jnp.bfloat16)


def per_device(features, out_grad, weight_mean, weight_noise, precision):
    feats = features[0, 0]
    grads = out_grad[0, 0]
    mean = weight_mean[0]
    prec = precision[0]
    cin = feats.shape[0]
    cout = grads.shape[0]
    kernel = noisy_weights(mean, weight_noise[0], prec, cout, cin)
    below = passed_along(feats[:, -1:], "space", 1)
    padded = jnp.pad(jnp.concatenate([below, feats], axis=1), ((0, 0), (0, 0), (1, 0), (1, 0)))
    preact = forward_conv(padded, kernel)
    activation = jax.nn.silu(preact).astype(jnp.bfloat16)
    act_in = passed_along(activation, "segment", 1)
    squash = jax.nn.sigmoid(preact)
    pre_grad = (grads.astype(jnp.float32) * squash * (1.0 + preact * (1.0 - squash))).astype(
        jnp.bfloat16
    )
    grad_in = passed_along(input_grad(pre_grad, kernel), "segment", -1)
    local_grad = weight_conv(padded, pre_grad)
    cell_count = (
        lax.axis_size("dp")
        * lax.axis_size("space")
        * pre_grad.shape[1]
        * pre_grad.shape[2]
        * pre_grad.shape[3]
    )
    inv_root = 1.0 / math.sqrt(cell_count)
    grad_total = lax.psum(local_grad.astype(jnp.bfloat16), ("dp", "space")).astype(jnp.float32)
    scaled = grad_total * inv_root
    prec_next = 0.75 * prec + 0.25 * scaled * scaled
    mean_new = mean - 0.03 * scaled / (prec_next + 0.1)
    return (act_in[None, None], grad_in[None, None], mean_new[None], prec_next[None])


def solution(mesh):
    in_specs = (
        P("dp", "segment", None, "space", None, None),
        P("dp", "segment", None, "space", None, None),
        P("segment", None, None),
        P("segment", None, None),
        P("segment", None, None),
    )
    out_specs = (
        P("dp", "segment", None, "space", None, None),
        P("dp", "segment", None, "space", None, None),
        P("segment", None, None),
        P("segment", None, None),
    )
    return jax.shard_map(
        per_device, mesh=mesh, in_specs=in_specs, out_specs=out_specs, check_vma=False
    )
```

profile of v0, /device:TPU:0, one launch (start us, length us, event | category | flops | bytes accessed | tf_op | source)
XLA Modules:
  0.0 176.4 jit_solution(7315777036722529213)
XLA Ops:
  7.2 0.9 slice.26
  8.1 4.9 %collective-permute-start = (bf16[32,1,6,256]{3,0,2,1:T(8,128)(2,1)S(1)}, bf16[32,1,6,256]{3,0,2,1:T(8,128)(2,1)S(1)}, u32[]{:S(2)}, u32[]{:S(2)}) collective-permute-start(bf16[32,1,6,256]{3,0,2,1:T(8,128)(2,1)S(1)} %slice.26), channel_id=1, source_target_pairs={{0,1},{1,2},{2,3},{4,5},{5,6},{6,7},{8,9},{9,10},{10,11},{12,13},{... | collective-permute-start | bytes 294920 | tf_op jit(solution)/shard_map/ppermute | solution.py:14
  13.1 2.0 %convert_reduce_fusion = bf16[27,2048]{1,0:T(8,128)(2,1)S(1)} fusion(f32[1,27,2048]{2,0,1:T(1,128)} %param.7, f32[1,27,2048]{2,0,1:T(1,128)} %param.8, f32[1,27,2048]{2,0,1:T(1,128)} %param.9), kind=kLoop, calls=%fused_computation.61 | loop fusion | flops 276480 | bytes 774144 | tf_op jit(solution)/shard_map/convert_element_type | solution.py:19
  15.1 1.1 reshape.121
  16.2 2.6 %fusion.55 = (bf16[32,1,7,7,257]{4,0,3,2,1:T(8,128)(2,1)}, bf16[32,7,7,1,257]{4,0,2,1,3:T(8,128)(2,1)S(1)}) fusion(bf16[32,6,6,256]{3,0,2,1:T(8,128)(2,1)} %bitcast.115, bf16[32,1,6,256]{3,0,2,1:T(8,128)(2,1)S(1)} %collective-permute-done), kind=kLoop, calls=%fused_computation.75 | loop fusion | flops 4432736 | bytes 2300032 | tf_op jit(solution)/shard_map/broadcast_in_dim | solution.py:49
  18.8 1.2 pad.5
  20.0 4.4 %reshape.91 = bf16[32,7,7,1,8,34]{5,4,0,2,1,3:T(8,128)(2,1)S(1)} reshape(bf16[32,7,7,1,272]{4,0,2,1,3:T(8,128)(2,1)} %pad.5) | data formatting | bytes 1705984 | tf_op jit(solution)/shard_map/conv_general_dilated | solution.py:24
  24.4 5.3 %copy.29 = bf16[32,7,7,1,8,34]{0,4,5,2,1,3:T(8,128)(2,1)} copy(bf16[32,7,7,1,8,34]{5,4,0,2,1,3:T(8,128)(2,1)S(1)} %reshape.91) | data formatting | bytes 1705984 | tf_op jit(solution)/shard_map/conv_general_dilated | solution.py:24
  29.6 1.0 slice.27
  30.6 4.3 %add_divide_fusion = (f32[3,3,8,17,64]{4,2,3,1,0:T(8,128)S(1)}, f32[3,3,8,17,64]{4,2,3,1,0:T(8,128)S(1)}, f32[3,3,8,17,64]{4,2,3,1,0:T(8,128)S(1)}) fusion(bf16[3,3,3,64,32]{4,3,2,1,0:T(8,128)(2,1)} %reshape.121, bf16[32,7,7,1,7,2]{0,4,5,2,1,3:T(8,128)(2,1)S(1)} %slice.27, bf16[32,7,7,1,8,34]{0,4,5,2,1,3:T(8,128)(2,1)} %copy.29, pred[8,17]{0,1:T(8,128)(4,1)S(1)} %copy-done.8), kind=kOutput, calls=%fused_computation.25 | convolution fusion | flops 138622464 | bytes 1947656 | tf_op jit(solution)/shard_map/conv_general_dilated | solution.py:24
  34.9 0.1 copy.32
  35.0 0.1 reshape.104
  35.2 0.2 copy.48
  35.4 0.1 copy.34
  35.5 0.1 reshape.106
  35.6 0.2 copy.49
  35.9 0.4 copy-done.6
  36.3 0.1 fusion.46
  36.4 0.2 copy.50
  36.6 0.1 pad.7.clone
  36.7 0.1 reshape.98
  36.9 0.1 copy.30
  37.0 0.1 reshape.95
  37.1 0.2 copy.47
  37.4 0.1 fusion.30
  37.5 1.7 copy.41
  39.2 13.4 %copy.40 = bf16[32,1,7,7,257]{0,1,4,3,2:T(2,128)(2,1)} copy(bf16[32,1,7,7,257]{4,0,3,2,1:T(8,128)(2,1)S(1)} %copy-done) | data formatting | bytes 1611904 | tf_op jit(solution)/shard_map/broadcast_in_dim | solution.py:49
  52.6 6.5 %broadcast_select_fusion = f32[7,7,8,34,32]{4,2,3,1,0:T(8,128)} fusion(pred[8,34]{0,1:T(8,128)(4,1)S(1)} %copy-done.7, bf16[3,3,3,64,32]{4,3,2,1,0:T(8,128)(2,1)S(1)} %copy-done.2, bf16[64,3,3,1,7,1]{0,4,5,2,1,3:T(8,128)(2,1)S(1)} %slice.31, bf16[64,3,3,1,8,17]{0,4,5,2,1,3:T(8,128)(2,1)S(1)} %copy.38), kind=kOutput, calls=%fused_computation.8 | convolution fusion | flops 136288768 | bytes 1981584 | tf_op jit(solution)/shard_map/conv_general_dilated | solution.py:36
  59.1 9.5 %copy.39 = f32[7,7,8,34,32]{3,2,4,1,0:T(8,128)} copy(f32[7,7,8,34,32]{4,2,3,1,0:T(8,128)} %broadcast_select_fusion) | data formatting | bytes 3411968 | tf_op jit(solution)/shard_map/conv_general_dilated | solution.py:36
  68.6 4.9 %reshape.102 = f32[7,7,1,272,32]{3,4,1,0,2:T(8,128)S(1)} reshape(f32[7,7,8,34,32]{3,2,4,1,0:T(8,128)} %copy.39) | data formatting | bytes 3411968 | tf_op jit(solution)/shard_map/conv_general_dilated | solution.py:36
  73.5 0.2 slice_bitcast_fusion
  73.7 0.1 slice_bitcast_fusion.1
  73.8 1.3 collective-permute-start.2
  75.1 15.4 %convolution_convert_fusion = bf16[3,3,3,64,32]{3,4,2,1,0:T(8,128)(2,1)S(1)} fusion(bf16[32,1,7,7,257]{0,1,4,3,2:T(2,128)(2,1)} %copy.40, bf16[64,1,3,3,128]{0,1,4,3,2:T(2,128)(2,1)S(1)} %copy-done.5), kind=kOutput, calls=%fused_computation.19 | convolution fusion | flops 127457280 | bytes 1064000 | tf_op jit(solution)/shard_map/transpose | solution.py:57
  90.6 0.2 slice.42
  90.8 0.3 copy.42
  91.0 1.2 convert_element_type.66
  92.2 1.1 fusion.44
  93.3 0.1 pad_maximum_fusion
  93.4 1.3 collective-permute-start.3
  94.7 0.1 fusion.38
  94.8 3.0 %collective-permute-start.1 = (bf16[64,3,3,128]{3,0,2,1:T(8,128)(2,1)S(1)}, bf16[64,3,3,128]{3,0,2,1:T(8,128)(2,1)S(1)}, u32[]{:S(2)}, u32[]{:S(2)}) collective-permute-start(bf16[64,3,3,128]{3,0,2,1:T(8,128)(2,1)S(1)} %fusion.38), channel_id=1, source_target_pairs={{0,4},{4,8},{8,12},{1,5},{5,9},{9,13},{2,6},{6,10},{10,14},{3,7},{... | collective-permute-start | bytes 442376 | tf_op jit(solution)/shard_map/ppermute | solution.py:14
  97.8 67.3 %all-reduce.3.cloned.1.call-done = bf16[27,2048]{1,0:T(8,128)(2,1)} async-done(((bf16[27,2048]{1,0:T(8,128)(2,1)}), bf16[27,2048]{1,0:T(8,128)(2,1)}) %all-reduce.3.cloned.1.call-update) | async-done | bytes 110608 | tf_op jit(solution)/shard_map/psum | solution.py:95
  165.2 1.1 fusion.47
  166.3 0.9 copy.45
  167.2 0.9 copy.44
  168.1 0.7 copy.62
  168.8 0.8 copy.63
  (28 shorter events, 0.3 us)
Async XLA Ops:
  7.2 158.0 %all-reduce.3.cloned.1.call-start = ((), (), s32[]{:S(2)}) async-start(), calls=%async_computation | async-start | bytes 262144 | tf_op jit(solution)/shard_map/psum | solution.py:95
  8.1 8.1 %collective-permute-start = (bf16[32,1,6,256]{3,0,2,1:T(8,128)(2,1)S(1)}, bf16[32,1,6,256]{3,0,2,1:T(8,128)(2,1)S(1)}, u32[]{:S(2)}, u32[]{:S(2)}) collective-permute-start(bf16[32,1,6,256]{3,0,2,1:T(8,128)(2,1)S(1)} %slice.26), channel_id=1, source_target_pairs={{0,1},{1,2},{2,3},{4,5},{5,6},{6,7},{8,9},{9,10},{10,11},{12,13},{... | collective-permute-start | bytes 294920 | tf_op jit(solution)/shard_map/ppermute | solution.py:14
  24.3 6.3 %copy-start.8 = (pred[8,17]{0,1:T(8,128)(4,1)S(1)}, pred[8,17]{0,1:T(8,128)(4,1)}, u32[]{:S(2)}) copy-start(pred[8,17]{0,1:T(8,128)(4,1)} %constant.36) | copy-start | bytes 412
  35.4 0.9 copy-start.6
  37.0 2.2 %copy-start = (bf16[32,1,7,7,257]{4,0,3,2,1:T(8,128)(2,1)S(1)}, bf16[32,1,7,7,257]{4,0,3,2,1:T(8,128)(2,1)}, u32[]{:S(2)}) copy-start(bf16[32,1,7,7,257]{4,0,3,2,1:T(8,128)(2,1)} %get-tuple-element.12) | copy-start | bytes 2417860
  39.2 13.4 %copy-start.2 = (bf16[3,3,3,64,32]{4,3,2,1,0:T(8,128)(2,1)S(1)}, bf16[3,3,3,64,32]{4,3,2,1,0:T(8,128)(2,1)}, u32[]{:S(2)}) copy-start(bf16[3,3,3,64,32]{4,3,2,1,0:T(8,128)(2,1)} %reshape.121) | copy-start | bytes 331780
  39.2 13.4 %copy-start.7 = (pred[8,34]{0,1:T(8,128)(4,1)S(1)}, pred[8,34]{0,1:T(8,128)(4,1)}, u32[]{:S(2)}) copy-start(pred[8,34]{0,1:T(8,128)(4,1)} %constant.37) | copy-start | bytes 820
  73.5 1.6 copy-start.5
  73.7 16.8 %copy-start.1 = (f32[32,7,7,257]{3,0,2,1:T(8,128)}, f32[32,7,7,257]{3,0,2,1:T(8,128)S(1)}, u32[]{:S(2)}) copy-start(f32[32,7,7,257]{3,0,2,1:T(8,128)S(1)} %slice_bitcast_fusion) | copy-start | bytes 4835716
  73.8 18.4 %collective-permute-start.2 = (f32[32,6,256]{2,0,1:T(8,128)S(1)}, f32[32,6,256]{2,0,1:T(8,128)S(1)}, u32[]{:S(2)}, u32[]{:S(2)}) collective-permute-start(f32[32,6,256]{2,0,1:T(8,128)S(1)} %slice_bitcast_fusion.1), channel_id=1, source_target_pairs={{1,0},{2,1},{3,2},{5,4},{6,5},{7,6},{9,8},{10,9},{11,10},{13,12},{... | collective-permute-start | bytes 589832 | tf_op jit(solution)/shard_map/ppermute | solution.py:14
  90.5 74.6 %copy-start.3 = (f32[1,27,2048]{2,0,1:T(1,128)S(1)}, f32[1,27,2048]{2,0,1:T(1,128)}, u32[]{:S(2)}) copy-start(f32[1,27,2048]{2,0,1:T(1,128)} %param.7) | copy-start | bytes 663556
  90.5 74.6 %copy-start.4 = (f32[1,27,2048]{2,0,1:T(1,128)S(1)}, f32[1,27,2048]{2,0,1:T(1,128)}, u32[]{:S(2)}) copy-start(f32[1,27,2048]{2,0,1:T(1,128)} %param.9) | copy-start | bytes 663556
  93.4 74.7 %collective-permute-start.3 = (bf16[32,6,6,256]{3,0,2,1:T(8,128)(2,1)S(1)}, bf16[32,6,6,256]{3,0,2,1:T(8,128)(2,1)S(1)}, u32[]{:S(2)}, u32[]{:S(2)}) collective-permute-start(bf16[32,6,6,256]{3,0,2,1:T(8,128)(2,1)S(1)} %pad_maximum_fusion), channel_id=1, source_target_pairs={{4,0},{8,4},{12,8},{5,1},{9,5},{13,9},{6,2},{10,6},{14,10},{7,3},{... | collective-permute-start | bytes 1769480 | tf_op jit(solution)/shard_map/ppermute | solution.py:14
  94.8 73.3 %collective-permute-start.1 = (bf16[64,3,3,128]{3,0,2,1:T(8,128)(2,1)S(1)}, bf16[64,3,3,128]{3,0,2,1:T(8,128)(2,1)S(1)}, u32[]{:S(2)}, u32[]{:S(2)}) collective-permute-start(bf16[64,3,3,128]{3,0,2,1:T(8,128)(2,1)S(1)} %fusion.38), channel_id=1, source_target_pairs={{0,4},{4,8},{8,12},{1,5},{5,9},{9,13},{2,6},{6,10},{10,14},{3,7},{... | collective-permute-start | bytes 442376 | tf_op jit(solution)/shard_map/ppermute | solution.py:14
Sparse Core Ops, SparseCore 0:
  92.3 72.7 all-reduce.2
where the time goes:
time: 177 us; the launch traced here: 176 us
  waiting for transfers between devices  67.4 us (38%)
  local copies, waits for them, and re-layouts  50.8 us (29%)
  matrix products  26.1 us (15%)
  between operations  14.3 us (8%)
  starting transfers between devices  10.6 us (6%)
  other arithmetic  7.14 us (4%)
    psum x1, waiting for transfers between devices, per_device(): lax.psum(local_grad.astype(jnp.bfloat16), ('dp', 'space'))  67.3 us
    transpose x1, matrix products, weight_conv(): return jnp.transpose(grads, (2, 3, 4, 1, 0)).reshape(27, -1)  15.4 us
    conv_general_dilated x5, local copies, waits for them, and re-layouts, input_conv(): lax.conv_general_dilated(pre_grad[None], flipped, (1, 1, 1), ((2, 2), (2,...  14.6 us
    broadcast_in_dim x1, local copies, waits for them, and re-layouts, weight_conv(): padded[:, None]  13.4 us
    conv_general_dilated x6, local copies, waits for them, and re-layouts, forward_conv(): lax.conv_general_dilated(padded[None], kernel, (2, 2, 2), 'VALID', dimens...  10.8 us
    ppermute x4, starting transfers between devices, passed_along(): return lax.ppermute(block, axis, route)  10.6 us
    conv_general_dilated x1, matrix products, input_conv(): lax.conv_general_dilated(pre_grad[None], flipped, (1, 1, 1), ((2, 2), (2,...  6.48 us
    unnamed x26, local copies, waits for them, and re-layouts  4.65 us
  transfers between devices with their start and end apart: 5, of which 1 were waited for; matrix products, arithmetic and copies ran while one was open for 14% of the time, Pallas kernels for 0%

commit v1 on v0

v1 whole, which is shorter than its diff:
```python
import functools
import math

import jax
import jax.numpy as jnp
from jax import lax
from jax.experimental import pallas as pl
from jax.experimental.pallas import tpu as pltpu
from jax.sharding import PartitionSpec as P

LANES = 128
TAPS = tuple((a, b, e) for a in range(3) for b in range(3) for e in range(3))
F32 = jnp.float32
BF16 = jnp.bfloat16


def passed_along(block, axis, distance):
    devices = range(lax.axis_size(axis))
    route = [(i - distance, i) for i in devices if i - distance in devices]
    return lax.ppermute(block, axis, route)


def matmul(a, b):
    return jnp.dot(a, b, preferred_element_type=F32)


def matmul_nt(a, b):
    return lax.dot_general(a, b, (((1,), (1,)), ((), ())), preferred_element_type=F32)


def iota(shape, dim):
    return lax.broadcasted_iota(jnp.int32, shape, dim)


def as_bf16(mask):
    return jnp.where(mask, 1.0, 0.0).astype(BF16)


def pick_strided(zs):
    half = zs // 2
    z = iota((zs, 3 * half), 0)
    n = iota((zs, 3 * half), 1)
    e = jnp.where(n >= 2 * half, 2, jnp.where(n >= half, 1, 0))
    return as_bf16(z == 2 * (n - e * half) + e - 1)


def spread_strided(zs):
    half = zs // 2
    row = iota((zs, zs), 0)
    z = iota((zs, zs), 1)
    p = jnp.where(row >= half, 1, 0)
    return as_bf16(z == 2 * (row - p * half) + p)


def regroup(cout, groups):
    per = cout // groups
    o = iota((cout, cout), 0)
    m = iota((cout, cout), 1)
    oi = jnp.zeros_like(m)
    for step in range(1, groups):
        oi = oi + jnp.where(m >= step * per, 1, 0)
    return as_bf16(o == (m - oi * per) * groups + oi)


def weight_matrix(noisy, cout, cin):
    groups = LANES // cin
    rows = cout // groups
    lane = iota((rows, LANES), 1)
    blocks = []
    for first in range(0, len(TAPS), groups):
        parts = []
        for oi in range(groups):
            part = jnp.zeros((rows, LANES), F32)
            for t in range(groups):
                if first + t >= len(TAPS):
                    continue
                tap = noisy[(first + t) * rows : (first + t + 1) * rows]
                shift = (t - oi) * cin % LANES
                tap = pltpu.roll(tap, shift, 1) if shift else tap
                keep = (lane >= t * cin) & (lane < (t + 1) * cin)
                part = jnp.where(keep, tap, part)
            parts.append(part)
        blocks.append(jnp.concatenate(parts, axis=0))
    mixed = jnp.concatenate(blocks, axis=1).astype(BF16)
    return matmul(regroup(cout, groups), mixed).astype(BF16)


def weight_rows(total, cout, cin):
    groups = LANES // cin
    rows = cout // groups
    lane = iota((rows, LANES), 1)
    mixed = lax.dot_general(
        regroup(cout, groups),
        total.astype(BF16),
        (((0,), (0,)), ((), ())),
        preferred_element_type=F32,
    )
    out = []
    for tap in range(len(TAPS)):
        t = tap % groups
        start = (tap // groups) * LANES
        row = jnp.zeros((rows, LANES), F32)
        for oi in range(groups):
            part = mixed[oi * rows : (oi + 1) * rows, start : start + LANES]
            shift = (oi - t) * cin % LANES
            part = pltpu.roll(part, shift, 1) if shift else part
            keep = (lane >= oi * cin) & (lane < (oi + 1) * cin)
            row = jnp.where(keep, part, row)
        out.append(row)
    return jnp.concatenate(out, axis=0).astype(BF16)


def forward_kernel(x_ref, halo_ref, g_ref, mean_ref, noise_ref, prec_ref,
                   act_ref, pre_ref, w_ref, dw_ref, col_ref):
    xd, ys, cin, zs = x_ref.shape
    ni, nj, cout, half = g_ref.shape
    width = w_ref.shape[1]
    noisy = mean_ref[...] + noise_ref[...] * lax.rsqrt(2000.0 * (prec_ref[...] + 0.1))
    weights = weight_matrix(noisy, cout, cin)
    w_ref[...] = weights
    pick = pick_strided(zs)
    col_ref[:, len(TAPS) * cin :, :] = jnp.zeros((ni, width - len(TAPS) * cin, nj * half), BF16)
    for x in range(-1, xd):
        plane = halo_ref[...] if x < 0 else x_ref[x]
        picked = matmul(plane.reshape(ys * cin, zs), pick).astype(BF16)
        for tap, (a, b, e) in enumerate(TAPS):
            i = (x + 1 - a) // 2
            if 2 * i + a - 1 != x or not 0 <= i < ni:
                continue
            for j in range(nj):
                y = 2 * j + b - 1
                if y < 0:
                    block = jnp.zeros((cin, half), BF16)
                else:
                    block = picked[y * cin : (y + 1) * cin, e * half : (e + 1) * half]
                col_ref[i, tap * cin : (tap + 1) * cin, j * half : (j + 1) * half] = block
    total = jnp.zeros((cout, width), F32)
    for i in range(ni):
        preact = matmul(weights, col_ref[i])
        squash = jax.nn.sigmoid(preact)
        act = (preact * squash).astype(BF16)
        for j in range(nj):
            act_ref[i, j] = act[:, j * half : (j + 1) * half]
        grads = jnp.concatenate([g_ref[i, j] for j in range(nj)], axis=1).astype(F32)
        pre = (grads * squash * (1.0 + preact * (1.0 - squash))).astype(BF16)
        pre_ref[i] = pre
        total = total + matmul_nt(pre, col_ref[i])
    dw_ref[...] = weight_rows(total, cout, cin)


def parity_taps(parity, shift):
    if parity == 0:
        return 1 if shift == 0 else None
    return 2 if shift == 0 else 0


def input_kernel(pre_ref, rim_ref, w_ref, out_ref, wt_ref, col_ref):
    xd, ys, cin, zs = out_ref.shape
    ni, cout, _ = pre_ref.shape
    half = zs // 2
    nj = ys // 2
    combos = [(p, q, r) for p in range(2) for q in range(2) for r in range(2)]
    flipped = jnp.transpose(
        jnp.concatenate([w_ref[...].astype(F32), jnp.zeros((LANES - cout, w_ref.shape[1]), F32)], axis=0)
    )
    for row, (px, py, pz) in enumerate(combos):
        for col, (di, dj) in enumerate((u, v) for u in range(2) for v in range(2)):
            pair = jnp.zeros((cin, LANES), F32)
            for dk in range(2):
                found = (parity_taps(px, di), parity_taps(py, dj), parity_taps(pz, dk))
                if None in found:
                    continue
                tap = TAPS.index(found)
                block = flipped[tap * cin : (tap + 1) * cin]
                pair = pair + (pltpu.roll(block, cout, 1) if dk else block)
            wt_ref[row * cin : (row + 1) * cin, col * LANES : (col + 1) * LANES] = pair.astype(BF16)
    last = iota((cout, half), 1) == half - 1
    for i in range(ni + 1):
        for j in range(nj + 1):
            if j == nj:
                here = jnp.zeros((cout, half), BF16)
                ahead = here
            else:
                source = rim_ref[...] if i == ni else pre_ref[i]
                here = source[:, j * half : (j + 1) * half]
                ahead = pltpu.roll(here.astype(F32), half - 1, 1)
                ahead = jnp.where(last, 0.0, ahead).astype(BF16)
            for di in range(2):
                for dj in range(2):
                    if not (0 <= i - di < ni and 0 <= j - dj < nj):
                        continue
                    row = (2 * di + dj) * 2 * cout
                    lane = ((i - di) * nj + j - dj) * half
                    col_ref[row : row + cout, lane : lane + half] = here
                    col_ref[row + cout : row + 2 * cout, lane : lane + half] = ahead
    spread = spread_strided(zs)
    for i in range(ni):
        for j in range(nj):
            lane = (i * nj + j) * half
            cells = matmul(wt_ref[...], col_ref[:, lane : lane + half]).astype(BF16)
            pairs = jnp.concatenate(
                [
                    jnp.concatenate(
                        [cells[(2 * n) * cin : (2 * n + 1) * cin], cells[(2 * n + 1) * cin : (2 * n + 2) * cin]],
                        axis=1,
                    )
                    for n in range(4)
                ],
                axis=0,
            )
            planes = matmul(pairs, spread).astype(BF16)
            for n in range(4):
                out_ref[2 * i + n // 2, 2 * j + n % 2] = planes[n * cin : (n + 1) * cin]


def add_up(block, axis):
    size = lax.axis_size(axis)
    if size & (size - 1):
        return lax.psum(block, axis)
    step = 1
    while step < size:
        other = lax.ppermute(block, axis, [(i, i ^ step) for i in range(size)])
        block = (block.astype(F32) + other.astype(F32)).astype(BF16)
        step *= 2
    return block


def per_device(features, out_grad, weight_mean, weight_noise, precision):
    feats = jnp.transpose(features[0, 0], (1, 2, 0, 3))
    grads = jnp.transpose(out_grad[0, 0], (1, 2, 0, 3))
    xd, ys, cin, zs = feats.shape
    ni, nj, cout, half = grads.shape
    flat = (weight_mean.size // LANES, LANES)
    mean = weight_mean.reshape(flat)
    prec = precision.reshape(flat)
    noise = weight_noise.reshape(flat)
    width = pl.cdiv(len(TAPS) * cin, LANES) * LANES

    below = passed_along(feats[xd - 1], "space", 1)
    act, pre, weights, dw = pl.pallas_call(
        forward_kernel,
        out_shape=(
            jax.ShapeDtypeStruct((ni, nj, cout, half), BF16),
            jax.ShapeDtypeStruct((ni, cout, nj * half), BF16),
            jax.ShapeDtypeStruct((cout, width), BF16),
            jax.ShapeDtypeStruct(flat, BF16),
        ),
        scratch_shapes=[pltpu.VMEM((ni, width, nj * half), BF16)],
        name="forward",
    )(feats, below, grads, mean, noise, prec)
    rim = passed_along(pre[0], "space", -1)
    act_in = passed_along(act, "segment", 1)
    spread_grad = pl.pallas_call(
        input_kernel,
        out_shape=jax.ShapeDtypeStruct((xd, ys, cin, zs), BF16),
        scratch_shapes=[
            pltpu.VMEM((8 * cin, 8 * cout), BF16),
            pltpu.VMEM((8 * cout, ni * nj * half), BF16),
        ],
        name="input_grad",
    )(pre, rim, weights)
    grad_in = passed_along(spread_grad, "segment", -1)

    cell_count = lax.axis_size("dp") * lax.axis_size("space") * ni * nj * half
    inv_root = 1.0 / math.sqrt(cell_count)
    grad_total = add_up(add_up(dw, "dp"), "space").astype(F32)
    scaled = grad_total * inv_root
    prec_next = 0.75 * prec + 0.25 * scaled * scaled
    mean_next = mean - 0.03 * scaled / (prec_next + 0.1)
    return (
        jnp.transpose(act_in, (2, 0, 1, 3))[None, None],
        jnp.transpose(grad_in, (2, 0, 1, 3))[None, None],
        mean_next.reshape(weight_mean.shape),
        prec_next.reshape(precision.shape),
    )


def solution(mesh):
    in_specs = (
        P("dp", "segment", None, "space", None, None),
        P("dp", "segment", None, "space", None, None),
        P("segment", None, None),
        P("segment", None, None),
        P("segment", None, None),
    )
    out_specs = (
        P("dp", "segment", None, "space", None, None),
        P("dp", "segment", None, "space", None, None),
        P("segment", None, None),
        P("segment", None, None),
    )
    return jax.shard_map(
        per_device, mesh=mesh, in_specs=in_specs, out_specs=out_specs, check_vma=False
    )
```

time: 177 us -> 46.3 us (0.26)
  waiting for transfers between devices: 67.4 us -> 15.5 us
  local copies, waits for them, and re-layouts: 50.8 us -> 4.44 us
  matrix products: 26.1 us -> 0 us
  between operations: 14.3 us -> 0.7 us
  Pallas kernels: 0 us -> 7.96 us
  other arithmetic: 7.14 us -> 1.82 us
  starting transfers between devices: 10.6 us -> 15.6 us
    psum x1 -> x0, waiting for transfers between devices: 67.3 us -> none  [per_device(): lax.psum(local_grad.astype(jnp.bfloat16), ('dp', 'space'))]
    conv_general_dilated x11 -> x0, local copies, waits for them, and re-layouts: 25.4 us -> none  [the longest x5 14.6 us: input_conv(): lax.conv_general_dilated(pre_grad[None], flipped, (1, 1, 1), ((2, 2), (2,...]
    transpose x1 -> x0, matrix products: 15.4 us -> none  [weight_conv(): return jnp.transpose(grads, (2, 3, 4, 1, 0)).reshape(27, -1)]
    broadcast_in_dim x2 -> x0, local copies, waits for them, and re-layouts: 14.6 us -> none  [the longest x1 13.4 us: weight_conv(): padded[:, None]]
    conv_general_dilated x2 -> x0, matrix products: 10.8 us -> none  [the longest x1 6.48 us: input_conv(): lax.conv_general_dilated(pre_grad[None], flipped, (1, 1, 1), ((2, 2), (2,...]
    ppermute x0 -> x3, waiting for transfers between devices: none -> 9.92 us  [add_up(): other = lax.ppermute(block, axis, [(i, i ^ step) for i in range(size)])]
    pallas_call x0 -> x2, Pallas kernels: none -> 7.96 us  [the longest x1 4.04 us: per_device(): pl.pallas_call(forward_kernel, out_shape=(jax.ShapeDtypeStruct((ni, nj, c...]
    ppermute x0 -> x3, starting transfers between devices: none -> 6.61 us  [add_up(): other = lax.ppermute(block, axis, [(i, i ^ step) for i in range(size)])]
  transfers between devices with their start and end apart: 5 -> 7, of which waited for: 1 -> 4; matrix products, arithmetic and copies ran while one was open for 14% -> 4% of each run, Pallas kernels for 0% -> 9%
where the time goes in v1:
time: 46.3 us; the launch traced here: 46 us
  starting transfers between devices  15.6 us (34%)
  waiting for transfers between devices  15.5 us (33%)
  Pallas kernels  7.96 us (17%)
  local copies, waits for them, and re-layouts  4.44 us (10%)
  other arithmetic  1.82 us (4%)
  between operations  0.7 us (2%)
    ppermute x3, waiting for transfers between devices, add_up(): other = lax.ppermute(block, axis, [(i, i ^ step) for i in range(size)])  9.92 us
    ppermute x4, starting transfers between devices, passed_along(): return lax.ppermute(block, axis, route)  8.94 us
    ppermute x3, starting transfers between devices, add_up(): other = lax.ppermute(block, axis, [(i, i ^ step) for i in range(size)])  6.61 us
    ppermute x4, waiting for transfers between devices, passed_along(): return lax.ppermute(block, axis, route)  5.56 us
    pallas_call x1, Pallas kernels, per_device(): pl.pallas_call(forward_kernel, out_shape=(jax.ShapeDtypeStruct((ni, nj, c...  4.04 us
    pallas_call x1, Pallas kernels, per_device(): pl.pallas_call(input_kernel, out_shape=jax.ShapeDtypeStruct((xd, ys, cin,...  3.92 us
    unnamed x12, local copies, waits for them, and re-layouts  2.73 us
    convert_element_type x2, other arithmetic, add_up(): block = (block.astype(F32) + other.astype(F32)).astype(BF16)  0.96 us
  transfers between devices with their start and end apart: 7, of which 4 were waited for; matrix products, arithmetic and copies ran while one was open for 4% of the time, Pallas kernels for 9%

profile of v1, /device:TPU:0, one launch (start us, length us, event | category | flops | bytes accessed | tf_op | source)
XLA Modules:
  0.0 46.0 jit_solution(15054837119007062621)
XLA Ops:
  0.6 0.9 %slice_bitcast_fusion = bf16[6,32,256]{2,1,0:T(8,128)(2,1)S(1)} fusion(bf16[6,6,32,256]{3,2,1,0:T(8,128)(2,1)} %bitcast.25), kind=kLoop, calls=%fused_computation.10 | loop fusion | bytes 196608 | tf_op jit(solution)/shard_map/squeeze | solution.py:239
  1.5 4.9 %collective-permute-start = (bf16[6,32,256]{2,1,0:T(8,128)(2,1)S(1)}, bf16[6,32,256]{2,1,0:T(8,128)(2,1)S(1)}, u32[]{:S(2)}, u32[]{:S(2)}) collective-permute-start(bf16[6,32,256]{2,1,0:T(8,128)(2,1)S(1)} %slice_bitcast_fusion), channel_id=1, source_target_pairs={{0,1},{1,2},{2,3},{4,5},{5,6},{6,7},{8,9},{9,10},{10,11},{12,13},{... | collective-permute-start | bytes 294920 | tf_op jit(solution)/shard_map/ppermute | solution.py:20
  6.5 2.2 %collective-permute-done.halo_ref = bf16[6,32,256]{2,1,0:T(8,128)(2,1)S(1)} collective-permute-done((bf16[6,32,256]{2,1,0:T(8,128)(2,1)S(1)}, bf16[6,32,256]{2,1,0:T(8,128)(2,1)S(1)}, u32[]{:S(2)}, u32[]{:S(2)}) %collective-permute-start) | collective-permute-done | bytes 98336 | tf_op jit(solution)/shard_map/ppermute | solution.py:20
  8.7 0.0 copy-start.2
  8.7 0.6 %copy-done.2 = bf16[6,32,256]{2,1,0:T(8,128)(2,1)} copy-done((bf16[6,32,256]{2,1,0:T(8,128)(2,1)}, bf16[6,32,256]{2,1,0:T(8,128)(2,1)S(1)}, u32[]{:S(2)}) %copy-start.2) | copy-done | bytes 98328
  9.3 4.0 %forward.1 = (bf16[3,3,64,128]{3,2,1,0:T(8,128)(2,1)}, bf16[3,64,384]{2,1,0:T(8,128)(2,1)}, bf16[64,896]{1,0:T(8,128)(2,1)}, bf16[432,128]{1,0:T(8,128)(2,1)}) custom-call(bf16[6,6,32,256]{3,2,1,0:T(8,128)(2,1)} %bitcast.26, bf16[6,32,256]{2,1,0:T(8,128)(2,1)} %copy-done.2, bf16[3,3,64,128]{3,2,1,0:T(8,128)(2,1)} %bitcast.31, f32[432,128]{1,0:T(8,128)} %bitcast.21, ...), custom_call_target="tpu_custom_call" | custom-call | tf_op jit(solution)/shard_map/forward/pallas_call | solution.py:240
  13.3 0.0 copy-start.4
  13.4 1.5 %collective-permute-start.4 = (bf16[432,128]{1,0:T(8,128)(2,1)}, bf16[432,128]{1,0:T(8,128)(2,1)S(1)}, u32[]{:S(2)}, u32[]{:S(2)}) collective-permute-start(bf16[432,128]{1,0:T(8,128)(2,1)} %get-tuple-element.11), channel_id=1, source_target_pairs={{0,16},{16,0},{1,17},{17,1},{2,18},{18,2},{3,19},{19,3},{4,20},{20... | collective-permute-start | bytes 331784 | tf_op jit(solution)/shard_map/ppermute | solution.py:222
  14.8 3.5 %collective-permute-done.4 = bf16[432,128]{1,0:T(8,128)(2,1)S(1)} collective-permute-done((bf16[432,128]{1,0:T(8,128)(2,1)}, bf16[432,128]{1,0:T(8,128)(2,1)S(1)}, u32[]{:S(2)}, u32[]{:S(2)}) %collective-permute-start.4) | collective-permute-done | bytes 110624 | tf_op jit(solution)/shard_map/ppermute | solution.py:222
  18.3 0.9 %add_convert_fusion.2 = bf16[432,128]{1,0:T(8,128)(2,1)S(1)} fusion(bf16[432,128]{1,0:T(8,128)(2,1)S(1)} %collective-permute-done.4, bf16[432,128]{1,0:T(8,128)(2,1)} %get-tuple-element.11), kind=kLoop, calls=%fused_computation.9 | loop fusion | flops 221184 | bytes 331776 | tf_op jit(solution)/shard_map/convert_element_type | solution.py:223
  19.2 2.5 %collective-permute-start.5 = (bf16[432,128]{1,0:T(8,128)(2,1)S(1)}, bf16[432,128]{1,0:T(8,128)(2,1)S(1)}, u32[]{:S(2)}, u32[]{:S(2)}) collective-permute-start(bf16[432,128]{1,0:T(8,128)(2,1)S(1)} %add_convert_fusion.2), channel_id=1, source_target_pairs={{0,1},{1,0},{2,3},{3,2},{4,5},{5,4},{6,7},{7,6},{8,9},{9,8},{10,11... | collective-permute-start | bytes 331784 | tf_op jit(solution)/shard_map/ppermute | solution.py:222
  21.7 0.8 %slice_bitcast_fusion.1 = bf16[64,384]{1,0:T(8,128)(2,1)S(1)} fusion(bf16[3,64,384]{2,1,0:T(8,128)(2,1)} %get-tuple-element.9.pre_ref), kind=kLoop, calls=%fused_computation.11 | loop fusion | bytes 98304 | tf_op jit(solution)/shard_map/squeeze | solution.py:251
  22.5 1.3 %collective-permute-start.2 = (bf16[64,384]{1,0:T(8,128)(2,1)S(1)}, bf16[64,384]{1,0:T(8,128)(2,1)S(1)}, u32[]{:S(2)}, u32[]{:S(2)}) collective-permute-start(bf16[64,384]{1,0:T(8,128)(2,1)S(1)} %slice_bitcast_fusion.1), channel_id=1, source_target_pairs={{1,0},{2,1},{3,2},{5,4},{6,5},{7,6},{9,8},{10,9},{11,10},{13,12},{... | collective-permute-start | bytes 147464 | tf_op jit(solution)/shard_map/ppermute | solution.py:20
  23.8 0.0 copy-done.4
  23.8 1.3 %collective-permute-start.1 = (bf16[3,3,64,128]{3,2,1,0:T(8,128)(2,1)S(1)}, bf16[3,3,64,128]{3,2,1,0:T(8,128)(2,1)S(1)}, u32[]{:S(2)}, u32[]{:S(2)}) collective-permute-start(bf16[3,3,64,128]{3,2,1,0:T(8,128)(2,1)S(1)} %copy-done.4), channel_id=1, source_target_pairs={{0,4},{4,8},{8,12},{1,5},{5,9},{9,13},{2,6},{6,10},{10,14},{3,7},{... | collective-permute-start | bytes 442376 | tf_op jit(solution)/shard_map/ppermute | solution.py:20
  25.1 3.4 %collective-permute-done.2.rim_ref = bf16[64,384]{1,0:T(8,128)(2,1)S(1)} collective-permute-done((bf16[64,384]{1,0:T(8,128)(2,1)S(1)}, bf16[64,384]{1,0:T(8,128)(2,1)S(1)}, u32[]{:S(2)}, u32[]{:S(2)}) %collective-permute-start.2) | collective-permute-done | bytes 49184 | tf_op jit(solution)/shard_map/ppermute | solution.py:20
  28.5 0.0 copy-start.3
  28.5 0.6 %copy-done.3 = bf16[64,384]{1,0:T(8,128)(2,1)} copy-done((bf16[64,384]{1,0:T(8,128)(2,1)}, bf16[64,384]{1,0:T(8,128)(2,1)S(1)}, u32[]{:S(2)}) %copy-start.3) | copy-done | bytes 49176
  29.1 0.0 copy-start.1
  29.1 3.9 %input_grad.1 = bf16[6,6,32,256]{3,2,1,0:T(8,128)(2,1)} custom-call(bf16[3,64,384]{2,1,0:T(8,128)(2,1)} %get-tuple-element.9.pre_ref, bf16[64,384]{1,0:T(8,128)(2,1)} %copy-done.3, bf16[64,896]{1,0:T(8,128)(2,1)} %get-tuple-element.10.w_ref), custom_call_target="tpu_custom_call" | custom-call | tf_op jit(solution)/shard_map/input_grad/pallas_call | solution.py:253
  33.0 0.0 copy-start
  33.0 1.4 %collective-permute-start.3 = (bf16[6,6,32,256]{3,2,1,0:T(8,128)(2,1)}, bf16[6,6,32,256]{3,2,1,0:T(8,128)(2,1)S(1)}, u32[]{:S(2)}, u32[]{:S(2)}) collective-permute-start(bf16[6,6,32,256]{3,2,1,0:T(8,128)(2,1)} %input_grad.1), channel_id=1, source_target_pairs={{4,0},{8,4},{12,8},{5,1},{9,5},{13,9},{6,2},{10,6},{14,10},{7,3},{... | collective-permute-start | bytes 1769480 | tf_op jit(solution)/shard_map/ppermute | solution.py:20
  34.5 0.0 collective-permute-done.5
  34.5 2.7 %collective-permute-start.6 = (bf16[432,128]{1,0:T(8,128)(2,1)S(1)}, bf16[432,128]{1,0:T(8,128)(2,1)S(1)}, u32[]{:S(2)}, u32[]{:S(2)}) collective-permute-start(bf16[432,128]{1,0:T(8,128)(2,1)S(1)} %add_convert_fusion.1), channel_id=1, source_target_pairs={{0,2},{1,3},{2,0},{3,1},{4,6},{5,7},{6,4},{7,5},{8,10},{9,11},{10,... | collective-permute-start | bytes 331784 | tf_op jit(solution)/shard_map/ppermute | solution.py:222
  37.2 0.0 collective-permute-done.1
  37.2 6.5 %collective-permute-done.6 = bf16[432,128]{1,0:T(8,128)(2,1)S(1)} collective-permute-done((bf16[432,128]{1,0:T(8,128)(2,1)S(1)}, bf16[432,128]{1,0:T(8,128)(2,1)S(1)}, u32[]{:S(2)}, u32[]{:S(2)}) %collective-permute-start.6) | collective-permute-done | bytes 110624 | tf_op jit(solution)/shard_map/ppermute | solution.py:222
  43.6 0.0 copy-done.1
  43.6 0.0 copy-done
  43.6 0.9 %fusion.3 = (f32[432,128]{1,0:T(8,128)}, f32[432,128]{1,0:T(8,128)}) fusion(f32[432,128]{1,0:T(8,128)S(1)} %bitcast.24, bf16[432,128]{1,0:T(8,128)(2,1)S(1)} %collective-permute-done.6, bf16[432,128]{1,0:T(8,128)(2,1)S(1)} %add_convert_fusion.1, f32[432,128]{1,0:T(8,128)S(1)} %bitcast.22), kind=kLoop, calls=%fused_computation.6 | loop fusion | flops 774144 | bytes 1105920 | tf_op jit(solution)/shard_map/add | solution.py:268
  44.5 0.0 collective-permute-done.3
  44.5 0.7 %copy.15 = bf16[1,1,64,3,3,128]{5,2,4,3,1,0:T(8,128)(2,1)} copy(bf16[1,1,64,3,3,128]{5,2,4,3,1,0:T(8,128)(2,1)S(1)} %bitcast.32) | data formatting | bytes 294912
  45.1 0.8 %copy.16 = bf16[1,1,32,6,6,256]{5,2,4,3,1,0:T(8,128)(2,1)} copy(bf16[1,1,32,6,6,256]{5,2,4,3,1,0:T(8,128)(2,1)S(1)} %bitcast.27) | data formatting | bytes 1179648
  (1 shorter events, 0.0 us)
Async XLA Ops:
  1.5 7.1 %collective-permute-start = (bf16[6,32,256]{2,1,0:T(8,128)(2,1)S(1)}, bf16[6,32,256]{2,1,0:T(8,128)(2,1)S(1)}, u32[]{:S(2)}, u32[]{:S(2)}) collective-permute-start(bf16[6,32,256]{2,1,0:T(8,128)(2,1)S(1)} %slice_bitcast_fusion), channel_id=1, source_target_pairs={{0,1},{1,2},{2,3},{4,5},{5,6},{6,7},{8,9},{9,10},{10,11},{12,13},{... | collective-permute-start | bytes 294920 | tf_op jit(solution)/shard_map/ppermute | solution.py:20
  8.7 0.6 %copy-start.2 = (bf16[6,32,256]{2,1,0:T(8,128)(2,1)}, bf16[6,32,256]{2,1,0:T(8,128)(2,1)S(1)}, u32[]{:S(2)}) copy-start(bf16[6,32,256]{2,1,0:T(8,128)(2,1)S(1)} %collective-permute-done.halo_ref) | copy-start | bytes 294916
  13.3 10.5 %copy-start.4 = (bf16[3,3,64,128]{3,2,1,0:T(8,128)(2,1)S(1)}, bf16[3,3,64,128]{3,2,1,0:T(8,128)(2,1)}, u32[]{:S(2)}) copy-start(bf16[3,3,64,128]{3,2,1,0:T(8,128)(2,1)} %get-tuple-element.8) | copy-start | bytes 442372
  13.4 5.0 %collective-permute-start.4 = (bf16[432,128]{1,0:T(8,128)(2,1)}, bf16[432,128]{1,0:T(8,128)(2,1)S(1)}, u32[]{:S(2)}, u32[]{:S(2)}) collective-permute-start(bf16[432,128]{1,0:T(8,128)(2,1)} %get-tuple-element.11), channel_id=1, source_target_pairs={{0,16},{16,0},{1,17},{17,1},{2,18},{18,2},{3,19},{19,3},{4,20},{20... | collective-permute-start | bytes 331784 | tf_op jit(solution)/shard_map/ppermute | solution.py:222
  19.2 15.2 %collective-permute-start.5 = (bf16[432,128]{1,0:T(8,128)(2,1)S(1)}, bf16[432,128]{1,0:T(8,128)(2,1)S(1)}, u32[]{:S(2)}, u32[]{:S(2)}) collective-permute-start(bf16[432,128]{1,0:T(8,128)(2,1)S(1)} %add_convert_fusion.2), channel_id=1, source_target_pairs={{0,1},{1,0},{2,3},{3,2},{4,5},{5,4},{6,7},{7,6},{8,9},{9,8},{10,11... | collective-permute-start | bytes 331784 | tf_op jit(solution)/shard_map/ppermute | solution.py:222
  22.5 6.0 %collective-permute-start.2 = (bf16[64,384]{1,0:T(8,128)(2,1)S(1)}, bf16[64,384]{1,0:T(8,128)(2,1)S(1)}, u32[]{:S(2)}, u32[]{:S(2)}) collective-permute-start(bf16[64,384]{1,0:T(8,128)(2,1)S(1)} %slice_bitcast_fusion.1), channel_id=1, source_target_pairs={{1,0},{2,1},{3,2},{5,4},{6,5},{7,6},{9,8},{10,9},{11,10},{13,12},{... | collective-permute-start | bytes 147464 | tf_op jit(solution)/shard_map/ppermute | solution.py:20
  23.8 13.3 %collective-permute-start.1 = (bf16[3,3,64,128]{3,2,1,0:T(8,128)(2,1)S(1)}, bf16[3,3,64,128]{3,2,1,0:T(8,128)(2,1)S(1)}, u32[]{:S(2)}, u32[]{:S(2)}) collective-permute-start(bf16[3,3,64,128]{3,2,1,0:T(8,128)(2,1)S(1)} %copy-done.4), channel_id=1, source_target_pairs={{0,4},{4,8},{8,12},{1,5},{5,9},{9,13},{2,6},{6,10},{10,14},{3,7},{... | collective-permute-start | bytes 442376 | tf_op jit(solution)/shard_map/ppermute | solution.py:20
  28.5 0.6 %copy-start.3 = (bf16[64,384]{1,0:T(8,128)(2,1)}, bf16[64,384]{1,0:T(8,128)(2,1)S(1)}, u32[]{:S(2)}) copy-start(bf16[64,384]{1,0:T(8,128)(2,1)S(1)} %collective-permute-done.2.rim_ref) | copy-start | bytes 147460
  29.1 14.5 %copy-start.1 = (f32[1,27,2048]{2,0,1:T(1,128)S(1)}, f32[1,27,2048]{2,0,1:T(1,128)}, u32[]{:S(2)}) copy-start(f32[1,27,2048]{2,0,1:T(1,128)} %param.9) | copy-start | bytes 663556
  33.0 10.6 %copy-start = (f32[1,27,2048]{2,0,1:T(1,128)S(1)}, f32[1,27,2048]{2,0,1:T(1,128)}, u32[]{:S(2)}) copy-start(f32[1,27,2048]{2,0,1:T(1,128)} %param.7) | copy-start | bytes 663556
  33.0 11.4 %collective-permute-start.3 = (bf16[6,6,32,256]{3,2,1,0:T(8,128)(2,1)}, bf16[6,6,32,256]{3,2,1,0:T(8,128)(2,1)S(1)}, u32[]{:S(2)}, u32[]{:S(2)}) collective-permute-start(bf16[6,6,32,256]{3,2,1,0:T(8,128)(2,1)} %input_grad.1), channel_id=1, source_target_pairs={{4,0},{8,4},{12,8},{5,1},{9,5},{13,9},{6,2},{10,6},{14,10},{7,3},{... | collective-permute-start | bytes 1769480 | tf_op jit(solution)/shard_map/ppermute | solution.py:20
  34.5 9.1 %collective-permute-start.6 = (bf16[432,128]{1,0:T(8,128)(2,1)S(1)}, bf16[432,128]{1,0:T(8,128)(2,1)S(1)}, u32[]{:S(2)}, u32[]{:S(2)}) collective-permute-start(bf16[432,128]{1,0:T(8,128)(2,1)S(1)} %add_convert_fusion.1), channel_id=1, source_target_pairs={{0,2},{1,3},{2,0},{3,1},{4,6},{5,7},{6,4},{7,5},{8,10},{9,11},{10,... | collective-permute-start | bytes 331784 | tf_op jit(solution)/shard_map/ppermute | solution.py:222

commit v2 on v1

--- a/solution.py
+++ b/solution.py
@@ -1,4 +1,3 @@
-import functools
 import math
 
 import jax
@@ -8,6 +7,7 @@
 from jax.experimental.pallas import tpu as pltpu
 from jax.sharding import PartitionSpec as P
 
+
 LANES = 128
 TAPS = tuple((a, b, e) for a in range(3) for b in range(3) for e in range(3))
 F32 = jnp.float32
@@ -26,6 +26,16 @@
 
 def matmul_nt(a, b):
     return lax.dot_general(a, b, (((1,), (1,)), ((), ())), preferred_element_type=F32)
+
+
+def passed_diagonally(block):
+    n_segment, n_space = lax.axis_size("segment"), lax.axis_size("space")
+    route = [
+        ((s + 1) * n_space + z + 1, s * n_space + z)
+        for s in range(n_segment - 1)
+        for z in range(n_space - 1)
+    ]
+    return lax.ppermute(block, ("segment", "space"), route)
 
 
 def iota(shape, dim):
@@ -110,42 +120,89 @@
     return jnp.concatenate(out, axis=0).astype(BF16)
 
 
-def forward_kernel(x_ref, halo_ref, g_ref, mean_ref, noise_ref, prec_ref,
-                   act_ref, pre_ref, w_ref, dw_ref, col_ref):
+def activate(preact, grads):
+    squash = jax.nn.sigmoid(preact)
+    act = (preact * squash).astype(BF16)
+    pre = (grads * squash * (1.0 + preact * (1.0 - squash))).astype(BF16)
+    return act, pre
+
+
+def place_plane(picked, x, ys, cin, half, targets):
+    for tap, (a, b, e) in enumerate(TAPS):
+        i = (x + 1 - a) // 2
+        if 2 * i + a - 1 != x or i not in targets:
+            continue
+        for j in range(ys // 2):
+            y = 2 * j + b - 1
+            if y < 0:
+                block = jnp.zeros((cin, half), BF16)
+            else:
+                block = picked[y * cin : (y + 1) * cin, e * half : (e + 1) * half]
+            targets[i][tap * cin : (tap + 1) * cin, j * half : (j + 1) * half] = block
+
+
+def prepare_kernel(x_hbm, g_hbm, mean_hbm, noise_hbm, prec_hbm,
+                   act_ref, pre_ref, w_ref, part_ref, total_ref, col_ref,
+                   x_ref, g_ref, mean_ref, noise_ref, prec_ref, cols_ref, sems):
     xd, ys, cin, zs = x_ref.shape
     ni, nj, cout, half = g_ref.shape
     width = w_ref.shape[1]
+    depth = len(TAPS) * cin
+    order = [pltpu.make_async_copy(x_hbm.at[x], x_ref.at[x], sems.at[x]) for x in range(xd)]
+    pairs = ((mean_hbm, mean_ref), (noise_hbm, noise_ref), (prec_hbm, prec_ref), (g_hbm, g_ref))
+    rest = [pltpu.make_async_copy(src, dst, sems.at[xd + n]) for n, (src, dst) in enumerate(pairs)]
+    for copy in order + rest:
+        copy.start()
+    targets = {0: col_ref, **{i: cols_ref.at[i - 1] for i in range(1, ni)}}
+    for ref in targets.values():
+        ref[depth:, :] = jnp.zeros((width - depth, nj * half), BF16)
+    pick = pick_strided(zs)
+    for x in range(xd):
+        order[x].wait()
+        picked = matmul(x_ref[x].reshape(ys * cin, zs), pick).astype(BF16)
+        place_plane(picked, x, ys, cin, half, targets)
+    for copy in rest:
+        copy.wait()
     noisy = mean_ref[...] + noise_ref[...] * lax.rsqrt(2000.0 * (prec_ref[...] + 0.1))
     weights = weight_matrix(noisy, cout, cin)
     w_ref[...] = weights
-    pick = pick_strided(zs)
-    col_ref[:, len(TAPS) * cin :, :] = jnp.zeros((ni, width - len(TAPS) * cin, nj * half), BF16)
-    for x in range(-1, xd):
-        plane = halo_ref[...] if x < 0 else x_ref[x]
-        picked = matmul(plane.reshape(ys * cin, zs), pick).astype(BF16)
-        for tap, (a, b, e) in enumerate(TAPS):
-            i = (x + 1 - a) // 2
-            if 2 * i + a - 1 != x or not 0 <= i < ni:
-                continue
-            for j in range(nj):
-                y = 2 * j + b - 1
-                if y < 0:
-                    block = jnp.zeros((cin, half), BF16)
-                else:
-                    block = picked[y * cin : (y + 1) * cin, e * half : (e + 1) * half]
-                col_ref[i, tap * cin : (tap + 1) * cin, j * half : (j + 1) * half] = block
     total = jnp.zeros((cout, width), F32)
-    for i in range(ni):
-        preact = matmul(weights, col_ref[i])
-        squash = jax.nn.sigmoid(preact)
-        act = (preact * squash).astype(BF16)
+    for i in range(1, ni):
+        preact = matmul(weights, cols_ref[i - 1])
+        grads = jnp.concatenate([g_ref[i, j] for j in range(nj)], axis=1).astype(F32)
+        act, pre = activate(preact, grads)
         for j in range(nj):
-            act_ref[i, j] = act[:, j * half : (j + 1) * half]
-        grads = jnp.concatenate([g_ref[i, j] for j in range(nj)], axis=1).astype(F32)
-        pre = (grads * squash * (1.0 + preact * (1.0 - squash))).astype(BF16)
-        pre_ref[i] = pre
-        total = total + matmul_nt(pre, col_ref[i])
-    dw_ref[...] = weight_rows(total, cout, cin)
+            act_ref[i - 1, j] = act[:, j * half : (j + 1) * half]
+        pre_ref[i - 1] = pre
+        total = total + matmul_nt(pre, cols_ref[i - 1])
+    total_ref[...] = total
+    first = depth // 3
+    part_ref[...] = matmul(weights[:, first:], col_ref[first:, :])
+
+
+def finish_kernel(halo_ref, act_rest_ref, pre_rest_ref, w_ref, part_ref, total_ref, col_in_ref, g_hbm,
+                  act_ref, pack_ref, rim_ref, dw_ref, col_ref, g_ref, sem):
+    ys, cin, zs = halo_ref.shape
+    ni, nj, cout, half = act_ref.shape
+    first = len(TAPS) * cin // 3
+    copy = pltpu.make_async_copy(g_hbm.at[0], g_ref, sem)
+    copy.start()
+    picked = matmul(halo_ref[...].reshape(ys * cin, zs), pick_strided(zs)).astype(BF16)
+    place_plane(picked, -1, ys, cin, half, {0: col_ref})
+    preact = part_ref[...] + matmul(w_ref[:, :first], col_ref[...])
+    copy.wait()
+    grads = jnp.concatenate([g_ref[j] for j in range(nj)], axis=1).astype(F32)
+    act, pre = activate(preact, grads)
+    for j in range(nj):
+        act_ref[0, j] = act[:, j * half : (j + 1) * half]
+    act_ref[1:] = act_rest_ref[...]
+    rim_ref[...] = pre
+    pack_ref[:, : nj * half] = pre
+    for i in range(1, ni):
+        pack_ref[:, i * nj * half : (i + 1) * nj * half] = pre_rest_ref[i - 1]
+    pack_ref[:, ni * nj * half :] = w_ref[...]
+    ours = jnp.concatenate([matmul_nt(pre, col_ref[...]), matmul_nt(pre, col_in_ref[first:, :])], axis=1)
+    dw_ref[...] = weight_rows(total_ref[...] + ours, cout, cin)
 
 
 def parity_taps(parity, shift):
@@ -154,14 +211,15 @@
     return 2 if shift == 0 else 0
 
 
-def input_kernel(pre_ref, rim_ref, w_ref, out_ref, wt_ref, col_ref):
+def input_kernel(pack_ref, rim_ref, out_ref, wt_ref, col_ref):
     xd, ys, cin, zs = out_ref.shape
-    ni, cout, _ = pre_ref.shape
+    cout = pack_ref.shape[0]
     half = zs // 2
-    nj = ys // 2
+    ni, nj = xd // 2, ys // 2
+    weights = pack_ref[:, ni * nj * half :]
     combos = [(p, q, r) for p in range(2) for q in range(2) for r in range(2)]
     flipped = jnp.transpose(
-        jnp.concatenate([w_ref[...].astype(F32), jnp.zeros((LANES - cout, w_ref.shape[1]), F32)], axis=0)
+        jnp.concatenate([weights.astype(F32), jnp.zeros((LANES - cout, weights.shape[1]), F32)], axis=0)
     )
     for row, (px, py, pz) in enumerate(combos):
         for col, (di, dj) in enumerate((u, v) for u in range(2) for v in range(2)):
@@ -181,8 +239,8 @@
                 here = jnp.zeros((cout, half), BF16)
                 ahead = here
             else:
-                source = rim_ref[...] if i == ni else pre_ref[i]
-                here = source[:, j * half : (j + 1) * half]
+                lane = (i * nj + j) * half
+                here = rim_ref[:, j * half : (j + 1) * half] if i == ni else pack_ref[:, lane : lane + half]
                 ahead = pltpu.roll(here.astype(F32), half - 1, 1)
                 ahead = jnp.where(last, 0.0, ahead).astype(BF16)
             for di in range(2):
@@ -213,19 +271,40 @@
                 out_ref[2 * i + n // 2, 2 * j + n % 2] = planes[n * cin : (n + 1) * cin]
 
 
-def add_up(block, axis):
-    size = lax.axis_size(axis)
-    if size & (size - 1):
-        return lax.psum(block, axis)
-    step = 1
-    while step < size:
-        other = lax.ppermute(block, axis, [(i, i ^ step) for i in range(size)])
+def copy_kernel(src_ref, out_ref):
+    out_ref[...] = src_ref[...]
+
+
+def swapped(block, flip_dp, flip_space):
+    n_space = lax.axis_size("space")
+    route = [
+        (d * n_space + s, (d ^ flip_dp) * n_space + (s ^ flip_space))
+        for d in range(lax.axis_size("dp"))
+        for s in range(n_space)
+    ]
+    return lax.ppermute(block, ("dp", "space"), route)
+
+
+def swap_totals(block):
+    n_dp, n_space = lax.axis_size("dp"), lax.axis_size("space")
+    if n_dp != 2 or n_space < 2 or n_space & (n_space - 1):
+        return lax.psum(block, ("dp", "space")).astype(F32)
+    stride = n_space // 2
+    while stride > 1:
+        other = swapped(block, 0, stride)
         block = (block.astype(F32) + other.astype(F32)).astype(BF16)
-        step *= 2
-    return block
-
-
-def per_device(features, out_grad, weight_mean, weight_noise, precision):
+        stride //= 2
+    both = swapped(block, 1, 1)
+    across = swapped(block, 1, 0)
+    beside = swapped(block, 0, 1)
+    return (block.astype(F32) + across.astype(F32)) + (beside.astype(F32) + both.astype(F32))
+
+
+def params(mib):
+    return pltpu.CompilerParams(vmem_limit_bytes=mib << 20)
+
+
+def step(features, out_grad, weight_mean, weight_noise, precision):
     feats = jnp.transpose(features[0, 0], (1, 2, 0, 3))
     grads = jnp.transpose(out_grad[0, 0], (1, 2, 0, 3))
     xd, ys, cin, zs = feats.shape
@@ -237,34 +316,71 @@
     width = pl.cdiv(len(TAPS) * cin, LANES) * LANES
 
     below = passed_along(feats[xd - 1], "space", 1)
-    act, pre, weights, dw = pl.pallas_call(
-        forward_kernel,
+    shape = jax.ShapeDtypeStruct
+    act_rest, pre_rest, weights, part, total, col = pl.pallas_call(
+        prepare_kernel,
         out_shape=(
-            jax.ShapeDtypeStruct((ni, nj, cout, half), BF16),
-            jax.ShapeDtypeStruct((ni, cout, nj * half), BF16),
-            jax.ShapeDtypeStruct((cout, width), BF16),
-            jax.ShapeDtypeStruct(flat, BF16),
+            shape((ni - 1, nj, cout, half), BF16),
+            shape((ni - 1, cout, nj * half), BF16),
+            shape((cout, width), BF16),
+            shape((cout, nj * half), F32),
+            shape((cout, width), F32),
+            shape((width, nj * half), BF16),
         ),
-        scratch_shapes=[pltpu.VMEM((ni, width, nj * half), BF16)],
-        name="forward",
-    )(feats, below, grads, mean, noise, prec)
-    rim = passed_along(pre[0], "space", -1)
+        in_specs=[pl.BlockSpec(memory_space=pltpu.HBM)] * 5,
+        scratch_shapes=[
+            pltpu.VMEM(feats.shape, BF16),
+            pltpu.VMEM(grads.shape, BF16),
+            pltpu.VMEM(flat, F32),
+            pltpu.VMEM(flat, F32),
+            pltpu.VMEM(flat, F32),
+            pltpu.VMEM((ni - 1, width, nj * half), BF16),
+            pltpu.SemaphoreType.DMA((xd + 4,)),
+        ],
+        compiler_params=params(24),
+        name="prepare",
+    )(*[pltpu.with_memory_space_constraint(v, pltpu.HBM) for v in (feats, grads, mean, noise, prec)])
+    vmem = pl.BlockSpec(memory_space=pltpu.VMEM)
+    act, pack, rim, dw = pl.pallas_call(
+        finish_kernel,
+        out_shape=(
+            shape((ni, nj, cout, half), BF16),
+            shape((cout, ni * nj * half + width), BF16),
+            shape((cout, nj * half), BF16),
+            shape(flat, BF16),
+        ),
+        in_specs=[vmem] * 7 + [pl.BlockSpec(memory_space=pltpu.HBM)],
+        scratch_shapes=[
+            pltpu.VMEM((len(TAPS) * cin // 3, nj * half), BF16),
+            pltpu.VMEM(grads.shape[1:], BF16),
+            pltpu.SemaphoreType.DMA,
+        ],
+        compiler_params=params(24),
+        name="finish",
+    )(below, act_rest, pre_rest, weights, part, total, col, grads)
+    pack = passed_along(pack, "segment", -1)
+    rim = passed_diagonally(rim)
     act_in = passed_along(act, "segment", 1)
-    spread_grad = pl.pallas_call(
+    grad_in = pl.pallas_call(
         input_kernel,
-        out_shape=jax.ShapeDtypeStruct((xd, ys, cin, zs), BF16),
+        out_shape=shape((xd, ys, cin, zs), BF16),
         scratch_shapes=[
             pltpu.VMEM((8 * cin, 8 * cout), BF16),
             pltpu.VMEM((8 * cout, ni * nj * half), BF16),
         ],
+        compiler_params=params(24),
         name="input_grad",
-    )(pre, rim, weights)
-    grad_in = passed_along(spread_grad, "segment", -1)
+    )(pack, rim)
+    act_in = pl.pallas_call(
+        copy_kernel,
+        out_shape=shape(act_in.shape, BF16),
+        compiler_params=params(8),
+        name="place",
+    )(act_in)
 
     cell_count = lax.axis_size("dp") * lax.axis_size("space") * ni * nj * half
     inv_root = 1.0 / math.sqrt(cell_count)
-    grad_total = add_up(add_up(dw, "dp"), "space").astype(F32)
-    scaled = grad_total * inv_root
+    scaled = swap_totals(dw) * inv_root
     prec_next = 0.75 * prec + 0.25 * scaled * scaled
     mean_next = mean - 0.03 * scaled / (prec_next + 0.1)
     return (
@@ -289,6 +405,4 @@
         P("segment", None, None),
         P("segment", None, None),
     )
-    return jax.shard_map(
-        per_device, mesh=mesh, in_specs=in_specs, out_specs=out_specs, check_vma=False
-    )
+    return jax.shard_map(step, mesh=mesh, in_specs=in_specs, out_specs=out_specs, check_vma=False)

time: 46.3 us -> 33.9 us (0.73)
  the two profiles are of different devices: /device:TPU:0 before, /device:TPU:1 now
where the time goes in v2:
time: 33.9 us; the launch traced here: 33.7 us
  starting transfers between devices  18.9 us (56%)
  Pallas kernels  8.12 us (24%)
  waiting for transfers between devices  4.09 us (12%)
  local copies, waits for them, and re-layouts  0.92 us (3%)
  other arithmetic  0.92 us (3%)
  between operations  0.75 us (2%)
    ppermute x3, starting transfers between devices, passed_along(): return lax.ppermute(block, axis, route)  12.5 us
    ppermute x4, starting transfers between devices, swapped(): return lax.ppermute(block, ('dp', 'space'), route)  5.09 us
    ppermute x1, waiting for transfers between devices, passed_diagonally(): return lax.ppermute(block, ('segment', 'space'), route)  3.42 us
    pallas_call x1, Pallas kernels, step(): pl.pallas_call(prepare_kernel, out_shape=(shape((ni - 1, nj, cout, half),...  3.39 us
    pallas_call x1, Pallas kernels, step(): pl.pallas_call(input_kernel, out_shape=shape((xd, ys, cin, zs), BF16), sc...  2.88 us
    ppermute x1, starting transfers between devices, passed_diagonally(): return lax.ppermute(block, ('segment', 'space'), route)  1.29 us
    pallas_call x1, Pallas kernels, step(): pl.pallas_call(finish_kernel, out_shape=(shape((ni, nj, cout, half), BF16...  1.18 us
    squeeze x1, local copies, waits for them, and re-layouts, step(): below = passed_along(feats[xd - 1], 'space', 1)  0.9 us
  transfers between devices with their start and end apart: 8, of which 2 were waited for; matrix products, arithmetic and copies ran while one was open for 3% of the time, Pallas kernels for 12%

profile of v2, /device:TPU:1, one launch (start us, length us, event | category | flops | bytes accessed | tf_op | source)
XLA Modules:
  0.0 33.7 jit_solution(9614133496880420726)
XLA Ops:
  0.6 0.9 %slice_bitcast_fusion = bf16[6,32,256]{2,1,0:T(8,128)(2,1)S(1)} fusion(bf16[6,6,32,256]{3,2,1,0:T(8,128)(2,1)} %bitcast.25), kind=kLoop, calls=%fused_computation.4 | loop fusion | bytes 196608 | tf_op jit(solution)/shard_map/squeeze | solution.py:318
  1.5 4.0 %collective-permute-start = (bf16[6,32,256]{2,1,0:T(8,128)(2,1)S(1)}, bf16[6,32,256]{2,1,0:T(8,128)(2,1)S(1)}, u32[]{:S(2)}, u32[]{:S(2)}) collective-permute-start(bf16[6,32,256]{2,1,0:T(8,128)(2,1)S(1)} %slice_bitcast_fusion), channel_id=1, source_target_pairs={{0,1},{1,2},{2,3},{4,5},{5,6},{6,7},{8,9},{9,10},{10,11},{12,13},{... | collective-permute-start | bytes 294920 | tf_op jit(solution)/shard_map/ppermute | solution.py:20
  5.6 0.0 copy-start
  5.6 3.4 %prepare.1 = (bf16[2,3,64,128]{3,2,1,0:T(8,128)(2,1)S(1)}, bf16[2,64,384]{2,1,0:T(8,128)(2,1)S(1)}, bf16[64,896]{1,0:T(8,128)(2,1)S(1)}, f32[64,384]{1,0:T(8,128...) custom-call(bf16[6,6,32,256]{3,2,1,0:T(8,128)(2,1)} %bitcast.26, bf16[3,3,64,128]{3,2,1,0:T(8,128)(2,1)} %bitcast.19, ...), custom_call_target="tpu_custom_call" | custom-call | tf_op jit(solution)/shard_map/prepare/pallas_call | solution.py:320
  9.0 0.0 collective-permute-done.halo_ref
  9.0 0.0 copy-done
  9.0 1.2 %finish.1 = (bf16[3,3,64,128]{3,2,1,0:T(8,128)(2,1)S(1)}, bf16[64,2048]{1,0:T(8,128)(2,1)S(1)}, bf16[64,384]{1,0:T(8,128)(2,1)S(1)}, bf16[432,128]{1,0:T(8,128)(2,1)S(1)}) custom-call(bf16[6,32,256]{2,1,0:T(8,128)(2,1)S(1)} %collective-permute-done.halo_ref, bf16[2,3,64,128]{3,2,1,0:T(8,128)(2,1)S(1)} %get-tuple-element.14.act_rest_ref, ...), custom_call_target="tpu_custom_call" | custom-call | tf_op jit(solution)/shard_map/finish/pallas_call | solution.py:344
  10.2 2.4 %collective-permute-start.4 = (bf16[432,128]{1,0:T(8,128)(2,1)S(1)}, bf16[432,128]{1,0:T(8,128)(2,1)S(1)}, u32[]{:S(2)}, u32[]{:S(2)}) collective-permute-start(bf16[432,128]{1,0:T(8,128)(2,1)S(1)} %get-tuple-element.23), channel_id=1, source_target_pairs={{0,2},{1,3},{2,0},{3,1},{16,18},{17,19},{18,16},{19,17},{4,6},{5,7... | collective-permute-start | bytes 331784 | tf_op jit(solution)/shard_map/ppermute | solution.py:285
  12.5 4.3 %collective-permute-start.1 = (bf16[3,3,64,128]{3,2,1,0:T(8,128)(2,1)S(1)}, bf16[3,3,64,128]{3,2,1,0:T(8,128)(2,1)S(1)}, u32[]{:S(2)}, u32[]{:S(2)}) collective-permute-start(bf16[3,3,64,128]{3,2,1,0:T(8,128)(2,1)S(1)} %get-tuple-element.20), channel_id=1, source_target_pairs={{0,4},{4,8},{8,12},{1,5},{5,9},{9,13},{2,6},{6,10},{10,14},{3,7},{... | collective-permute-start | bytes 442376 | tf_op jit(solution)/shard_map/ppermute | solution.py:20
  16.8 0.7 %collective-permute-done.4 = bf16[432,128]{1,0:T(8,128)(2,1)S(1)} collective-permute-done((bf16[432,128]{1,0:T(8,128)(2,1)S(1)}, bf16[432,128]{1,0:T(8,128)(2,1)S(1)}, u32[]{:S(2)}, u32[]{:S(2)}) %collective-permute-start.4) | collective-permute-done | bytes 110624 | tf_op jit(solution)/shard_map/ppermute | solution.py:285
  17.5 0.0 copy-start.2
  17.5 0.0 copy-start.1
  17.5 1.2 %collective-permute-start.7 = (bf16[432,128]{1,0:T(8,128)(2,1)S(1)}, bf16[432,128]{1,0:T(8,128)(2,1)S(1)}, u32[]{:S(2)}, u32[]{:S(2)}) collective-permute-start(bf16[432,128]{1,0:T(8,128)(2,1)S(1)} %add_convert_fusion), channel_id=1, source_target_pairs={{0,17},{1,16},{2,19},{3,18},{16,1},{17,0},{18,3},{19,2},{4,21},{5,... | collective-permute-start | bytes 331784 | tf_op jit(solution)/shard_map/ppermute | solution.py:285
  18.7 1.3 %collective-permute-start.6 = (bf16[432,128]{1,0:T(8,128)(2,1)S(1)}, bf16[432,128]{1,0:T(8,128)(2,1)S(1)}, u32[]{:S(2)}, u32[]{:S(2)}) collective-permute-start(bf16[432,128]{1,0:T(8,128)(2,1)S(1)} %add_convert_fusion), channel_id=1, source_target_pairs={{0,1},{1,0},{2,3},{3,2},{16,17},{17,16},{18,19},{19,18},{4,5},{5,4... | collective-permute-start | bytes 331784 | tf_op jit(solution)/shard_map/ppermute | solution.py:285
  20.0 0.2 collective-permute-start.5
  20.2 4.2 %collective-permute-start.2 = (bf16[64,2048]{1,0:T(8,128)(2,1)S(1)}, bf16[64,2048]{1,0:T(8,128)(2,1)S(1)}, u32[]{:S(2)}, u32[]{:S(2)}) collective-permute-start(bf16[64,2048]{1,0:T(8,128)(2,1)S(1)} %get-tuple-element.21), channel_id=1, source_target_pairs={{4,0},{8,4},{12,8},{5,1},{9,5},{13,9},{6,2},{10,6},{14,10},{7,3},{... | collective-permute-start | bytes 786440 | tf_op jit(solution)/shard_map/ppermute | solution.py:20
  24.5 0.0 collective-permute-done.1.src_ref
  24.5 1.3 %collective-permute-start.3 = (bf16[64,384]{1,0:T(8,128)(2,1)S(1)}, bf16[64,384]{1,0:T(8,128)(2,1)S(1)}, u32[]{:S(2)}, u32[]{:S(2)}) collective-permute-start(bf16[64,384]{1,0:T(8,128)(2,1)S(1)} %get-tuple-element.22), channel_id=1, source_target_pairs={{5,0},{6,1},{7,2},{9,4},{10,5},{11,6},{13,8},{14,9},{15,10},{21,16... | collective-permute-start | bytes 147464 | tf_op jit(solution)/shard_map/ppermute | solution.py:38
  25.8 0.7 %place.1 = bf16[3,3,64,128]{3,2,1,0:T(8,128)(2,1)} custom-call(bf16[3,3,64,128]{3,2,1,0:T(8,128)(2,1)S(1)} %collective-permute-done.1.src_ref), custom_call_target="tpu_custom_call" | custom-call | tf_op jit(solution)/shard_map/place/pallas_call | solution.py:374
  26.5 0.0 collective-permute-done.7
  26.5 0.0 collective-permute-done.6
  26.5 0.0 collective-permute-done.5
  26.5 0.0 copy-done.2
  26.5 0.0 copy-done.1
  26.5 0.9 %multiply_add_fusion = (f32[432,128]{1,0:T(8,128)}, f32[432,128]{1,0:T(8,128)}) fusion(f32[432,128]{1,0:T(8,128)S(1)} %bitcast.24, bf16[432,128]{1,0:T(8,128)(2,1)S(1)} %collective-permute-done.7, bf16[432,128]{1,0:T(8,128)(2,1)S(1)} %collective-permute-done.6, bf16[432,128]{1,0:T(8,128)(2,1)S(1)} %collective-permute-done.5, ...), kind=kLoop, calls=%fused_computation.1 | loop fusion | flops 884736 | bytes 1327104 | tf_op jit(solution)/shard_map/add | solution.py:384
  27.4 3.4 %collective-permute-done.3.rim_ref = bf16[64,384]{1,0:T(8,128)(2,1)S(1)} collective-permute-done((bf16[64,384]{1,0:T(8,128)(2,1)S(1)}, bf16[64,384]{1,0:T(8,128)(2,1)S(1)}, u32[]{:S(2)}, u32[]{:S(2)}) %collective-permute-start.3) | collective-permute-done | bytes 49184 | tf_op jit(solution)/shard_map/ppermute | solution.py:38
  30.8 0.0 collective-permute-done.2.pack_ref
  30.8 2.9 %input_grad.1 = bf16[6,6,32,256]{3,2,1,0:T(8,128)(2,1)} custom-call(bf16[64,2048]{1,0:T(8,128)(2,1)S(1)} %collective-permute-done.2.pack_ref, bf16[64,384]{1,0:T(8,128)(2,1)S(1)} %collective-permute-done.3.rim_ref), custom_call_target="tpu_custom_call" | custom-call | tf_op jit(solution)/shard_map/input_grad/pallas_call | solution.py:364
  (1 shorter events, 0.0 us)
Async XLA Ops:
  1.5 7.4 %collective-permute-start = (bf16[6,32,256]{2,1,0:T(8,128)(2,1)S(1)}, bf16[6,32,256]{2,1,0:T(8,128)(2,1)S(1)}, u32[]{:S(2)}, u32[]{:S(2)}) collective-permute-start(bf16[6,32,256]{2,1,0:T(8,128)(2,1)S(1)} %slice_bitcast_fusion), channel_id=1, source_target_pairs={{0,1},{1,2},{2,3},{4,5},{5,6},{6,7},{8,9},{9,10},{10,11},{12,13},{... | collective-permute-start | bytes 294920 | tf_op jit(solution)/shard_map/ppermute | solution.py:20
  5.6 3.4 %copy-start = (bf16[1,1,64,3,3,128]{5,2,4,3,1,0:T(8,128)(2,1)S(1)}, bf16[1,1,64,3,3,128]{5,2,4,3,1,0:T(8,128)(2,1)}, u32[]{:S(2)}) copy-start(bf16[1,1,64,3,3,128]{5,2,4,3,1,0:T(8,128)(2,1)} %param.6) | copy-start | bytes 442372
  10.2 7.3 %collective-permute-start.4 = (bf16[432,128]{1,0:T(8,128)(2,1)S(1)}, bf16[432,128]{1,0:T(8,128)(2,1)S(1)}, u32[]{:S(2)}, u32[]{:S(2)}) collective-permute-start(bf16[432,128]{1,0:T(8,128)(2,1)S(1)} %get-tuple-element.23), channel_id=1, source_target_pairs={{0,2},{1,3},{2,0},{3,1},{16,18},{17,19},{18,16},{19,17},{4,6},{5,7... | collective-permute-start | bytes 331784 | tf_op jit(solution)/shard_map/ppermute | solution.py:285
  12.5 11.9 %collective-permute-start.1 = (bf16[3,3,64,128]{3,2,1,0:T(8,128)(2,1)S(1)}, bf16[3,3,64,128]{3,2,1,0:T(8,128)(2,1)S(1)}, u32[]{:S(2)}, u32[]{:S(2)}) collective-permute-start(bf16[3,3,64,128]{3,2,1,0:T(8,128)(2,1)S(1)} %get-tuple-element.20), channel_id=1, source_target_pairs={{0,4},{4,8},{8,12},{1,5},{5,9},{9,13},{2,6},{6,10},{10,14},{3,7},{... | collective-permute-start | bytes 442376 | tf_op jit(solution)/shard_map/ppermute | solution.py:20
  17.5 9.0 %copy-start.2 = (f32[1,27,2048]{2,0,1:T(1,128)S(1)}, f32[1,27,2048]{2,0,1:T(1,128)}, u32[]{:S(2)}) copy-start(f32[1,27,2048]{2,0,1:T(1,128)} %param.9) | copy-start | bytes 663556
  17.5 9.0 %copy-start.1 = (f32[1,27,2048]{2,0,1:T(1,128)S(1)}, f32[1,27,2048]{2,0,1:T(1,128)}, u32[]{:S(2)}) copy-start(f32[1,27,2048]{2,0,1:T(1,128)} %param.7) | copy-start | bytes 663556
  17.5 9.0 %collective-permute-start.7 = (bf16[432,128]{1,0:T(8,128)(2,1)S(1)}, bf16[432,128]{1,0:T(8,128)(2,1)S(1)}, u32[]{:S(2)}, u32[]{:S(2)}) collective-permute-start(bf16[432,128]{1,0:T(8,128)(2,1)S(1)} %add_convert_fusion), channel_id=1, source_target_pairs={{0,17},{1,16},{2,19},{3,18},{16,1},{17,0},{18,3},{19,2},{4,21},{5,... | collective-permute-start | bytes 331784 | tf_op jit(solution)/shard_map/ppermute | solution.py:285
  18.7 7.7 %collective-permute-start.6 = (bf16[432,128]{1,0:T(8,128)(2,1)S(1)}, bf16[432,128]{1,0:T(8,128)(2,1)S(1)}, u32[]{:S(2)}, u32[]{:S(2)}) collective-permute-start(bf16[432,128]{1,0:T(8,128)(2,1)S(1)} %add_convert_fusion), channel_id=1, source_target_pairs={{0,1},{1,0},{2,3},{3,2},{16,17},{17,16},{18,19},{19,18},{4,5},{5,4... | collective-permute-start | bytes 331784 | tf_op jit(solution)/shard_map/ppermute | solution.py:285
  20.0 6.5 %collective-permute-start.5 = (bf16[432,128]{1,0:T(8,128)(2,1)S(1)}, bf16[432,128]{1,0:T(8,128)(2,1)S(1)}, u32[]{:S(2)}, u32[]{:S(2)}) collective-permute-start(bf16[432,128]{1,0:T(8,128)(2,1)S(1)} %add_convert_fusion), channel_id=1, source_target_pairs={{0,16},{1,17},{2,18},{3,19},{16,0},{17,1},{18,2},{19,3},{4,20},{5,... | collective-permute-start | bytes 331784 | tf_op jit(solution)/shard_map/ppermute | solution.py:285
  20.2 10.6 %collective-permute-start.2 = (bf16[64,2048]{1,0:T(8,128)(2,1)S(1)}, bf16[64,2048]{1,0:T(8,128)(2,1)S(1)}, u32[]{:S(2)}, u32[]{:S(2)}) collective-permute-start(bf16[64,2048]{1,0:T(8,128)(2,1)S(1)} %get-tuple-element.21), channel_id=1, source_target_pairs={{4,0},{8,4},{12,8},{5,1},{9,5},{13,9},{6,2},{10,6},{14,10},{7,3},{... | collective-permute-start | bytes 786440 | tf_op jit(solution)/shard_map/ppermute | solution.py:20
  24.5 6.3 %collective-permute-start.3 = (bf16[64,384]{1,0:T(8,128)(2,1)S(1)}, bf16[64,384]{1,0:T(8,128)(2,1)S(1)}, u32[]{:S(2)}, u32[]{:S(2)}) collective-permute-start(bf16[64,384]{1,0:T(8,128)(2,1)S(1)} %get-tuple-element.22), channel_id=1, source_target_pairs={{5,0},{6,1},{7,2},{9,4},{10,5},{11,6},{13,8},{14,9},{15,10},{21,16... | collective-permute-start | bytes 147464 | tf_op jit(solution)/shard_map/ppermute | solution.py:38

commit v3 on v2

--- a/solution.py
+++ b/solution.py
@@ -14,10 +14,22 @@
 BF16 = jnp.bfloat16
 
 
-def passed_along(block, axis, distance):
-    devices = range(lax.axis_size(axis))
-    route = [(i - distance, i) for i in devices if i - distance in devices]
-    return lax.ppermute(block, axis, route)
+def passed_along(block, steps):
+    axes = tuple(steps)
+    route = [(0, 0)]
+    for axis in axes:
+        size = lax.axis_size(axis)
+        route = [
+            (src * size + i, dst * size + (i + steps[axis]) % size)
+            for src, dst in route
+            for i in range(size)
+        ]
+    return lax.ppermute(block, axes, route)
+
+
+def unless(axis, end):
+    last = lax.axis_size(axis) - 1 if end else 0
+    return jnp.where(lax.axis_index(axis) == last, 0.0, 1.0)
 
 
 def matmul(a, b):
@@ -26,16 +38,6 @@
 
 def matmul_nt(a, b):
     return lax.dot_general(a, b, (((1,), (1,)), ((), ())), preferred_element_type=F32)
-
-
-def passed_diagonally(block):
-    n_segment, n_space = lax.axis_size("segment"), lax.axis_size("space")
-    route = [
-        ((s + 1) * n_space + z + 1, s * n_space + z)
-        for s in range(n_segment - 1)
-        for z in range(n_space - 1)
-    ]
-    return lax.ppermute(block, ("segment", "space"), route)
 
 
 def iota(shape, dim):
@@ -187,7 +189,8 @@
     first = len(TAPS) * cin // 3
     copy = pltpu.make_async_copy(g_hbm.at[0], g_ref, sem)
     copy.start()
-    picked = matmul(halo_ref[...].reshape(ys * cin, zs), pick_strided(zs)).astype(BF16)
+    picked = matmul(halo_ref[...].reshape(ys * cin, zs), pick_strided(zs))
+    picked = (picked * unless("space", 0)).astype(BF16)
     place_plane(picked, -1, ys, cin, half, {0: col_ref})
     preact = part_ref[...] + matmul(w_ref[:, :first], col_ref[...])
     copy.wait()
@@ -211,15 +214,20 @@
     return 2 if shift == 0 else 0
 
 
-def input_kernel(pack_ref, rim_ref, out_ref, wt_ref, col_ref):
+def input_kernel(pack_ref, rim_ref, act_ref, out_hbm, act_hbm,
+                 wt_ref, col_ref, out_ref, act_out_ref, sems):
     xd, ys, cin, zs = out_ref.shape
+    act_out_ref[...] = (act_ref[...].astype(F32) * unless("segment", 0)).astype(BF16)
+    copies = [pltpu.make_async_copy(act_out_ref, act_hbm, sems.at[xd // 2])]
+    copies[0].start()
     cout = pack_ref.shape[0]
     half = zs // 2
     ni, nj = xd // 2, ys // 2
-    weights = pack_ref[:, ni * nj * half :]
+    weights = pack_ref[:, ni * nj * half :].astype(F32) * unless("segment", 1)
+    rim = (rim_ref[...].astype(F32) * unless("space", 1)).astype(BF16)
     combos = [(p, q, r) for p in range(2) for q in range(2) for r in range(2)]
     flipped = jnp.transpose(
-        jnp.concatenate([weights.astype(F32), jnp.zeros((LANES - cout, weights.shape[1]), F32)], axis=0)
+        jnp.concatenate([weights, jnp.zeros((LANES - cout, weights.shape[1]), F32)], axis=0)
     )
     for row, (px, py, pz) in enumerate(combos):
         for col, (di, dj) in enumerate((u, v) for u in range(2) for v in range(2)):
@@ -240,7 +248,7 @@
                 ahead = here
             else:
                 lane = (i * nj + j) * half
-                here = rim_ref[:, j * half : (j + 1) * half] if i == ni else pack_ref[:, lane : lane + half]
+                here = rim[:, j * half : (j + 1) * half] if i == ni else pack_ref[:, lane : lane + half]
                 ahead = pltpu.roll(here.astype(F32), half - 1, 1)
                 ahead = jnp.where(last, 0.0, ahead).astype(BF16)
             for di in range(2):
@@ -269,10 +277,12 @@
             planes = matmul(pairs, spread).astype(BF16)
             for n in range(4):
                 out_ref[2 * i + n // 2, 2 * j + n % 2] = planes[n * cin : (n + 1) * cin]
-
-
-def copy_kernel(src_ref, out_ref):
-    out_ref[...] = src_ref[...]
+        copies.append(
+            pltpu.make_async_copy(out_ref.at[2 * i : 2 * i + 2], out_hbm.at[2 * i : 2 * i + 2], sems.at[i])
+        )
+        copies[-1].start()
+    for copy in copies:
+        copy.wait()
 
 
 def swapped(block, flip_dp, flip_space):
@@ -315,7 +325,7 @@
     noise = weight_noise.reshape(flat)
     width = pl.cdiv(len(TAPS) * cin, LANES) * LANES
 
-    below = passed_along(feats[xd - 1], "space", 1)
+    below = passed_along(feats[xd - 1], {"space": 1})
     shape = jax.ShapeDtypeStruct
     act_rest, pre_rest, weights, part, total, col = pl.pallas_call(
         prepare_kernel,
@@ -358,25 +368,25 @@
         compiler_params=params(24),
         name="finish",
     )(below, act_rest, pre_rest, weights, part, total, col, grads)
-    pack = passed_along(pack, "segment", -1)
-    rim = passed_diagonally(rim)
-    act_in = passed_along(act, "segment", 1)
-    grad_in = pl.pallas_call(
+    pack = passed_along(pack, {"segment": -1})
+    rim = passed_along(rim, {"segment": -1, "space": -1})
+    act_in = passed_along(act, {"segment": 1})
+    hbm = pl.BlockSpec(memory_space=pltpu.HBM)
+    grad_in, act_in = pl.pallas_call(
         input_kernel,
-        out_shape=shape((xd, ys, cin, zs), BF16),
+        out_shape=(shape((xd, ys, cin, zs), BF16), shape(act.shape, BF16)),
+        in_specs=[vmem] * 3,
+        out_specs=(hbm, hbm),
         scratch_shapes=[
             pltpu.VMEM((8 * cin, 8 * cout), BF16),
             pltpu.VMEM((8 * cout, ni * nj * half), BF16),
+            pltpu.VMEM((xd, ys, cin, zs), BF16),
+            pltpu.VMEM(act.shape, BF16),
+            pltpu.SemaphoreType.DMA((ni + 1,)),
         ],
         compiler_params=params(24),
         name="input_grad",
-    )(pack, rim)
-    act_in = pl.pallas_call(
-        copy_kernel,
-        out_shape=shape(act_in.shape, BF16),
-        compiler_params=params(8),
-        name="place",
-    )(act_in)
+    )(pack, rim, act_in)
 
     cell_count = lax.axis_size("dp") * lax.axis_size("space") * ni * nj * half
     inv_root = 1.0 / math.sqrt(cell_count)

time: 33.9 us -> 32.6 us (0.962)
  the two profiles are of different devices: /device:TPU:1 before, /device:TPU:0 now
where the time goes in v3:
time: 32.6 us; the launch traced here: 32.4 us
  waiting for transfers between devices  12.2 us (37%)
  starting transfers between devices  10.3 us (32%)
  Pallas kernels  7.42 us (23%)
  other arithmetic  0.93 us (3%)
  local copies, waits for them, and re-layouts  0.92 us (3%)
  between operations  0.68 us (2%)
    ppermute x4, waiting for transfers between devices, swapped(): return lax.ppermute(block, ('dp', 'space'), route)  8.42 us
    ppermute x4, starting transfers between devices, passed_along(): return lax.ppermute(block, axes, route)  5.45 us
    ppermute x4, starting transfers between devices, swapped(): return lax.ppermute(block, ('dp', 'space'), route)  4.83 us
    ppermute x4, waiting for transfers between devices, passed_along(): return lax.ppermute(block, axes, route)  3.8 us
    pallas_call x1, Pallas kernels, step(): pl.pallas_call(prepare_kernel, out_shape=(shape((ni - 1, nj, cout, half),...  3.39 us
    pallas_call x1, Pallas kernels, step(): pl.pallas_call(input_kernel, out_shape=(shape((xd, ys, cin, zs), BF16), s...  2.86 us
    pallas_call x1, Pallas kernels, step(): pl.pallas_call(finish_kernel, out_shape=(shape((ni, nj, cout, half), BF16...  1.17 us
    squeeze x1, local copies, waits for them, and re-layouts, step(): below = passed_along(feats[xd - 1], {'space': 1})  0.9 us
  transfers between devices with their start and end apart: 8, of which 6 were waited for; matrix products, arithmetic and copies ran while one was open for 3% of the time, Pallas kernels for 10%

profile of v3, /device:TPU:0, one launch (start us, length us, event | category | flops | bytes accessed | tf_op | source)
XLA Modules:
  0.0 32.4 jit_solution(16154438413071158631)
XLA Ops:
  0.6 0.9 %slice_bitcast_fusion = bf16[6,32,256]{2,1,0:T(8,128)(2,1)S(1)} fusion(bf16[6,6,32,256]{3,2,1,0:T(8,128)(2,1)} %bitcast.25), kind=kLoop, calls=%fused_computation.4 | loop fusion | bytes 196608 | tf_op jit(solution)/shard_map/squeeze | solution.py:328
  1.5 3.1 %collective-permute-start = (bf16[6,32,256]{2,1,0:T(8,128)(2,1)S(1)}, bf16[6,32,256]{2,1,0:T(8,128)(2,1)S(1)}, u32[]{:S(2)}, u32[]{:S(2)}) collective-permute-start(bf16[6,32,256]{2,1,0:T(8,128)(2,1)S(1)} %slice_bitcast_fusion), channel_id=1, source_target_pairs={{0,1},{1,2},{2,3},{3,0},{4,5},{5,6},{6,7},{7,4},{8,9},{9,10},{10,1... | collective-permute-start | bytes 294920 | tf_op jit(solution)/shard_map/ppermute | solution.py:27
  4.6 0.0 copy-start
  4.6 3.4 %prepare.1 = (bf16[2,3,64,128]{3,2,1,0:T(8,128)(2,1)S(1)}, bf16[2,64,384]{2,1,0:T(8,128)(2,1)S(1)}, bf16[64,896]{1,0:T(8,128)(2,1)S(1)}, f32[64,384]{1,0:T(8,128...) custom-call(bf16[6,6,32,256]{3,2,1,0:T(8,128)(2,1)} %bitcast.26, bf16[3,3,64,128]{3,2,1,0:T(8,128)(2,1)} %bitcast.19, ...), custom_call_target="tpu_custom_call" | custom-call | tf_op jit(solution)/shard_map/prepare/pallas_call | solution.py:330
  8.0 1.4 %collective-permute-done.halo_ref = bf16[6,32,256]{2,1,0:T(8,128)(2,1)S(1)} collective-permute-done((bf16[6,32,256]{2,1,0:T(8,128)(2,1)S(1)}, bf16[6,32,256]{2,1,0:T(8,128)(2,1)S(1)}, u32[]{:S(2)}, u32[]{:S(2)}) %collective-permute-start) | collective-permute-done | bytes 98336 | tf_op jit(solution)/shard_map/ppermute | solution.py:27
  9.4 0.0 copy-done
  9.4 0.0 copy-start.2
  9.4 1.2 %finish.1 = (bf16[3,3,64,128]{3,2,1,0:T(8,128)(2,1)S(1)}, bf16[64,2048]{1,0:T(8,128)(2,1)S(1)}, bf16[64,384]{1,0:T(8,128)(2,1)S(1)}, bf16[432,128]{1,0:T(8,128)(2,1)S(1)}) custom-call(bf16[6,32,256]{2,1,0:T(8,128)(2,1)S(1)} %collective-permute-done.halo_ref, bf16[2,3,64,128]{3,2,1,0:T(8,128)(2,1)S(1)} %get-tuple-element.16.act_rest_ref, ...), custom_call_target="tpu_custom_call" | custom-call | tf_op jit(solution)/shard_map/finish/pallas_call | solution.py:354
  10.6 0.0 copy-start.1
  10.6 1.3 %collective-permute-start.4 = (bf16[432,128]{1,0:T(8,128)(2,1)S(1)}, bf16[432,128]{1,0:T(8,128)(2,1)S(1)}, u32[]{:S(2)}, u32[]{:S(2)}) collective-permute-start(bf16[432,128]{1,0:T(8,128)(2,1)S(1)} %get-tuple-element.27), channel_id=1, source_target_pairs={{0,2},{1,3},{2,0},{3,1},{16,18},{17,19},{18,16},{19,17},{4,6},{5,7... | collective-permute-start | bytes 331784 | tf_op jit(solution)/shard_map/ppermute | solution.py:295
  11.9 6.2 %collective-permute-done.4 = bf16[432,128]{1,0:T(8,128)(2,1)S(1)} collective-permute-done((bf16[432,128]{1,0:T(8,128)(2,1)S(1)}, bf16[432,128]{1,0:T(8,128)(2,1)S(1)}, u32[]{:S(2)}, u32[]{:S(2)}) %collective-permute-start.4) | collective-permute-done | bytes 110624 | tf_op jit(solution)/shard_map/ppermute | solution.py:295
  18.1 0.1 collective-permute-start.7
  18.2 2.5 %collective-permute-start.6 = (bf16[432,128]{1,0:T(8,128)(2,1)S(1)}, bf16[432,128]{1,0:T(8,128)(2,1)S(1)}, u32[]{:S(2)}, u32[]{:S(2)}) collective-permute-start(bf16[432,128]{1,0:T(8,128)(2,1)S(1)} %add_convert_fusion), channel_id=1, source_target_pairs={{0,1},{1,0},{2,3},{3,2},{16,17},{17,16},{18,19},{19,18},{4,5},{5,4... | collective-permute-start | bytes 331784 | tf_op jit(solution)/shard_map/ppermute | solution.py:295
  20.7 1.0 %collective-permute-start.5 = (bf16[432,128]{1,0:T(8,128)(2,1)S(1)}, bf16[432,128]{1,0:T(8,128)(2,1)S(1)}, u32[]{:S(2)}, u32[]{:S(2)}) collective-permute-start(bf16[432,128]{1,0:T(8,128)(2,1)S(1)} %add_convert_fusion), channel_id=1, source_target_pairs={{0,16},{1,17},{2,18},{3,19},{16,0},{17,1},{18,2},{19,3},{4,20},{5,... | collective-permute-start | bytes 331784 | tf_op jit(solution)/shard_map/ppermute | solution.py:295
  21.7 0.0 collective-permute-start.1
  21.7 2.4 %collective-permute-start.2 = (bf16[64,384]{1,0:T(8,128)(2,1)S(1)}, bf16[64,384]{1,0:T(8,128)(2,1)S(1)}, u32[]{:S(2)}, u32[]{:S(2)}) collective-permute-start(bf16[64,384]{1,0:T(8,128)(2,1)S(1)} %get-tuple-element.23), channel_id=1, source_target_pairs={{0,15},{1,12},{2,13},{3,14},{4,3},{5,0},{6,1},{7,2},{8,7},{9,4},{1... | collective-permute-start | bytes 147464 | tf_op jit(solution)/shard_map/ppermute | solution.py:27
  24.1 0.9 %collective-permute-done.7 = bf16[432,128]{1,0:T(8,128)(2,1)S(1)} collective-permute-done((bf16[432,128]{1,0:T(8,128)(2,1)S(1)}, bf16[432,128]{1,0:T(8,128)(2,1)S(1)}, u32[]{:S(2)}, u32[]{:S(2)}) %collective-permute-start.7) | collective-permute-done | bytes 110624 | tf_op jit(solution)/shard_map/ppermute | solution.py:295
  25.0 0.0 collective-permute-start.3
  25.0 1.0 %collective-permute-done.6 = bf16[432,128]{1,0:T(8,128)(2,1)S(1)} collective-permute-done((bf16[432,128]{1,0:T(8,128)(2,1)S(1)}, bf16[432,128]{1,0:T(8,128)(2,1)S(1)}, u32[]{:S(2)}, u32[]{:S(2)}) %collective-permute-start.6) | collective-permute-done | bytes 110624 | tf_op jit(solution)/shard_map/ppermute | solution.py:295
  26.0 0.3 collective-permute-done.5
  26.3 0.0 copy-done.2
  26.3 0.0 copy-done.1
  26.3 0.9 %multiply_add_fusion = (f32[432,128]{1,0:T(8,128)}, f32[432,128]{1,0:T(8,128)}) fusion(f32[432,128]{1,0:T(8,128)S(1)} %bitcast.24, bf16[432,128]{1,0:T(8,128)(2,1)S(1)} %collective-permute-done.7, bf16[432,128]{1,0:T(8,128)(2,1)S(1)} %collective-permute-done.6, bf16[432,128]{1,0:T(8,128)(2,1)S(1)} %collective-permute-done.5, ...), kind=kLoop, calls=%fused_computation.1 | loop fusion | flops 884736 | bytes 1327104 | tf_op jit(solution)/shard_map/add | solution.py:394
  27.2 0.0 collective-permute-done.2.rim_ref
  27.2 2.4 %collective-permute-done.3.act_ref = bf16[3,3,64,128]{3,2,1,0:T(8,128)(2,1)S(1)} collective-permute-done((bf16[3,3,64,128]{3,2,1,0:T(8,128)(2,1)S(1)}, bf16[3,3,64,128]{3,2,1,0:T(8,128)(2,1)S(1)}, u32[]{:S(2)}, u32[]{:S(2)}) %collective-permute-start.3) | collective-permute-done | bytes 147488 | tf_op jit(solution)/shard_map/ppermute | solution.py:27
  29.6 0.0 collective-permute-done.1.pack_ref
  29.6 2.9 %input_grad.1 = (bf16[6,6,32,256]{3,2,1,0:T(8,128)(2,1)}, bf16[3,3,64,128]{3,2,1,0:T(8,128)(2,1)}) custom-call(bf16[64,2048]{1,0:T(8,128)(2,1)S(1)} %collective-permute-done.1.pack_ref, bf16[64,384]{1,0:T(8,128)(2,1)S(1)} %collective-permute-done.2.rim_ref, bf16[3,3,64,128]{3,2,1,0:T(8,128)(2,1)S(1)} %collective-permute-done.3.act_ref), custom_call_target="tpu_custom_call" | custom-call | tf_op jit(solution)/shard_map/input_grad/pallas_call | solution.py:375
  (1 shorter events, 0.0 us)
Async XLA Ops:
  1.5 7.9 %collective-permute-start = (bf16[6,32,256]{2,1,0:T(8,128)(2,1)S(1)}, bf16[6,32,256]{2,1,0:T(8,128)(2,1)S(1)}, u32[]{:S(2)}, u32[]{:S(2)}) collective-permute-start(bf16[6,32,256]{2,1,0:T(8,128)(2,1)S(1)} %slice_bitcast_fusion), channel_id=1, source_target_pairs={{0,1},{1,2},{2,3},{3,0},{4,5},{5,6},{6,7},{7,4},{8,9},{9,10},{10,1... | collective-permute-start | bytes 294920 | tf_op jit(solution)/shard_map/ppermute | solution.py:27
  4.6 4.8 %copy-start = (bf16[1,1,64,3,3,128]{5,2,4,3,1,0:T(8,128)(2,1)S(1)}, bf16[1,1,64,3,3,128]{5,2,4,3,1,0:T(8,128)(2,1)}, u32[]{:S(2)}) copy-start(bf16[1,1,64,3,3,128]{5,2,4,3,1,0:T(8,128)(2,1)} %param.6) | copy-start | bytes 442372
  9.4 16.9 %copy-start.2 = (f32[1,27,2048]{2,0,1:T(1,128)S(1)}, f32[1,27,2048]{2,0,1:T(1,128)}, u32[]{:S(2)}) copy-start(f32[1,27,2048]{2,0,1:T(1,128)} %param.9) | copy-start | bytes 663556
  10.6 15.7 %copy-start.1 = (f32[1,27,2048]{2,0,1:T(1,128)S(1)}, f32[1,27,2048]{2,0,1:T(1,128)}, u32[]{:S(2)}) copy-start(f32[1,27,2048]{2,0,1:T(1,128)} %param.7) | copy-start | bytes 663556
  10.6 7.5 %collective-permute-start.4 = (bf16[432,128]{1,0:T(8,128)(2,1)S(1)}, bf16[432,128]{1,0:T(8,128)(2,1)S(1)}, u32[]{:S(2)}, u32[]{:S(2)}) collective-permute-start(bf16[432,128]{1,0:T(8,128)(2,1)S(1)} %get-tuple-element.27), channel_id=1, source_target_pairs={{0,2},{1,3},{2,0},{3,1},{16,18},{17,19},{18,16},{19,17},{4,6},{5,7... | collective-permute-start | bytes 331784 | tf_op jit(solution)/shard_map/ppermute | solution.py:295
  18.1 6.9 %collective-permute-start.7 = (bf16[432,128]{1,0:T(8,128)(2,1)S(1)}, bf16[432,128]{1,0:T(8,128)(2,1)S(1)}, u32[]{:S(2)}, u32[]{:S(2)}) collective-permute-start(bf16[432,128]{1,0:T(8,128)(2,1)S(1)} %add_convert_fusion), channel_id=1, source_target_pairs={{0,17},{1,16},{2,19},{3,18},{16,1},{17,0},{18,3},{19,2},{4,21},{5,... | collective-permute-start | bytes 331784 | tf_op jit(solution)/shard_map/ppermute | solution.py:295
  18.2 7.8 %collective-permute-start.6 = (bf16[432,128]{1,0:T(8,128)(2,1)S(1)}, bf16[432,128]{1,0:T(8,128)(2,1)S(1)}, u32[]{:S(2)}, u32[]{:S(2)}) collective-permute-start(bf16[432,128]{1,0:T(8,128)(2,1)S(1)} %add_convert_fusion), channel_id=1, source_target_pairs={{0,1},{1,0},{2,3},{3,2},{16,17},{17,16},{18,19},{19,18},{4,5},{5,4... | collective-permute-start | bytes 331784 | tf_op jit(solution)/shard_map/ppermute | solution.py:295
  20.7 5.6 %collective-permute-start.5 = (bf16[432,128]{1,0:T(8,128)(2,1)S(1)}, bf16[432,128]{1,0:T(8,128)(2,1)S(1)}, u32[]{:S(2)}, u32[]{:S(2)}) collective-permute-start(bf16[432,128]{1,0:T(8,128)(2,1)S(1)} %add_convert_fusion), channel_id=1, source_target_pairs={{0,16},{1,17},{2,18},{3,19},{16,0},{17,1},{18,2},{19,3},{4,20},{5,... | collective-permute-start | bytes 331784 | tf_op jit(solution)/shard_map/ppermute | solution.py:295
  21.7 7.9 %collective-permute-start.1 = (bf16[64,2048]{1,0:T(8,128)(2,1)S(1)}, bf16[64,2048]{1,0:T(8,128)(2,1)S(1)}, u32[]{:S(2)}, u32[]{:S(2)}) collective-permute-start(bf16[64,2048]{1,0:T(8,128)(2,1)S(1)} %get-tuple-element.22), channel_id=1, source_target_pairs={{0,12},{4,0},{8,4},{12,8},{1,13},{5,1},{9,5},{13,9},{2,14},{6,2},{... | collective-permute-start | bytes 786440 | tf_op jit(solution)/shard_map/ppermute | solution.py:27
  21.7 5.5 %collective-permute-start.2 = (bf16[64,384]{1,0:T(8,128)(2,1)S(1)}, bf16[64,384]{1,0:T(8,128)(2,1)S(1)}, u32[]{:S(2)}, u32[]{:S(2)}) collective-permute-start(bf16[64,384]{1,0:T(8,128)(2,1)S(1)} %get-tuple-element.23), channel_id=1, source_target_pairs={{0,15},{1,12},{2,13},{3,14},{4,3},{5,0},{6,1},{7,2},{8,7},{9,4},{1... | collective-permute-start | bytes 147464 | tf_op jit(solution)/shard_map/ppermute | solution.py:27
  25.0 4.6 %collective-permute-start.3 = (bf16[3,3,64,128]{3,2,1,0:T(8,128)(2,1)S(1)}, bf16[3,3,64,128]{3,2,1,0:T(8,128)(2,1)S(1)}, u32[]{:S(2)}, u32[]{:S(2)}) collective-permute-start(bf16[3,3,64,128]{3,2,1,0:T(8,128)(2,1)S(1)} %get-tuple-element.24), channel_id=1, source_target_pairs={{0,4},{4,8},{8,12},{12,0},{1,5},{5,9},{9,13},{13,1},{2,6},{6,10},{... | collective-permute-start | bytes 442376 | tf_op jit(solution)/shard_map/ppermute | solution.py:27

commit v4 on v3

--- a/solution.py
+++ b/solution.py
@@ -9,7 +9,8 @@
 
 
 LANES = 128
-TAPS = tuple((a, b, e) for a in range(3) for b in range(3) for e in range(3))
+TAPS = tuple((a, b, e) for a in (1, 2, 0) for b in range(3) for e in range(3))
+STORED = tuple(9 * a + 3 * b + e for a, b, e in TAPS)
 F32 = jnp.float32
 BF16 = jnp.bfloat16
 
@@ -64,10 +65,10 @@
     return as_bf16(z == 2 * (row - p * half) + p)
 
 
-def regroup(cout, groups):
+def regroup(cout, groups, back=False):
     per = cout // groups
-    o = iota((cout, cout), 0)
-    m = iota((cout, cout), 1)
+    o = iota((cout, cout), 0 if back else 1)
+    m = iota((cout, cout), 1 if back else 0)
     oi = jnp.zeros_like(m)
     for step in range(1, groups):
         oi = oi + jnp.where(m >= step * per, 1, 0)
@@ -86,34 +87,29 @@
             for t in range(groups):
                 if first + t >= len(TAPS):
                     continue
-                tap = noisy[(first + t) * rows : (first + t + 1) * rows]
+                stored = STORED[first + t]
+                tap = noisy[stored * rows : (stored + 1) * rows]
                 shift = (t - oi) * cin % LANES
                 tap = pltpu.roll(tap, shift, 1) if shift else tap
                 keep = (lane >= t * cin) & (lane < (t + 1) * cin)
                 part = jnp.where(keep, tap, part)
             parts.append(part)
         blocks.append(jnp.concatenate(parts, axis=0))
-    mixed = jnp.concatenate(blocks, axis=1).astype(BF16)
-    return matmul(regroup(cout, groups), mixed).astype(BF16)
+    return jnp.concatenate(blocks, axis=1).astype(BF16)
 
 
 def weight_rows(total, cout, cin):
     groups = LANES // cin
     rows = cout // groups
     lane = iota((rows, LANES), 1)
-    mixed = lax.dot_general(
-        regroup(cout, groups),
-        total.astype(BF16),
-        (((0,), (0,)), ((), ())),
-        preferred_element_type=F32,
-    )
     out = []
-    for tap in range(len(TAPS)):
+    for stored in range(len(TAPS)):
+        tap = STORED.index(stored)
         t = tap % groups
         start = (tap // groups) * LANES
         row = jnp.zeros((rows, LANES), F32)
         for oi in range(groups):
-            part = mixed[oi * rows : (oi + 1) * rows, start : start + LANES]
+            part = total[oi * rows : (oi + 1) * rows, start : start + LANES]
             shift = (oi - t) * cin % LANES
             part = pltpu.roll(part, shift, 1) if shift else part
             keep = (lane >= oi * cin) & (lane < (oi + 1) * cin)
@@ -129,7 +125,7 @@
     return act, pre
 
 
-def place_plane(picked, x, ys, cin, half, targets):
+def place_plane(picked, x, ys, cin, half, targets, first=0):
     for tap, (a, b, e) in enumerate(TAPS):
         i = (x + 1 - a) // 2
         if 2 * i + a - 1 != x or i not in targets:
@@ -140,11 +136,30 @@
                 block = jnp.zeros((cin, half), BF16)
             else:
                 block = picked[y * cin : (y + 1) * cin, e * half : (e + 1) * half]
-            targets[i][tap * cin : (tap + 1) * cin, j * half : (j + 1) * half] = block
+            row = tap * cin - first
+            targets[i][row : row + cin, j * half : (j + 1) * half] = block
+
+
+def plane_kernel(x_hbm, out_ref, sem):
+    last = lax.axis_index("space") == lax.axis_size("space") - 1
+
+    @pl.when(last)
+    def _():
+        out_ref[...] = jnp.zeros(out_ref.shape, out_ref.dtype)
+
+    @pl.when(jnp.logical_not(last))
+    def _():
+        copy = pltpu.make_async_copy(x_hbm.at[x_hbm.shape[0] - 1], out_ref, sem)
+        copy.start()
+        copy.wait()
+
+
+def tail_rows(cin):
+    return 2 * len(TAPS) * cin // 3 // LANES * LANES
 
 
 def prepare_kernel(x_hbm, g_hbm, mean_hbm, noise_hbm, prec_hbm,
-                   act_ref, pre_ref, w_ref, part_ref, total_ref, col_ref,
+                   act_ref, pre_ref, w_ref, part_ref, total_ref, col_ref, pick_ref, g0_ref,
                    x_ref, g_ref, mean_ref, noise_ref, prec_ref, cols_ref, sems):
     xd, ys, cin, zs = x_ref.shape
     ni, nj, cout, half = g_ref.shape
@@ -159,53 +174,60 @@
     for ref in targets.values():
         ref[depth:, :] = jnp.zeros((width - depth, nj * half), BF16)
     pick = pick_strided(zs)
-    for x in range(xd):
+    pick_ref[...] = pick
+    there, back = regroup(cout, LANES // cin), regroup(cout, LANES // cin, True)
+    for x in range(0, xd, 2):
         order[x].wait()
-        picked = matmul(x_ref[x].reshape(ys * cin, zs), pick).astype(BF16)
-        place_plane(picked, x, ys, cin, half, targets)
+        order[x + 1].wait()
+        picked = matmul(x_ref[x : x + 2].reshape(2 * ys * cin, zs), pick).astype(BF16)
+        place_plane(picked[: ys * cin], x, ys, cin, half, targets)
+        place_plane(picked[ys * cin :], x + 1, ys, cin, half, targets)
     for copy in rest:
         copy.wait()
     noisy = mean_ref[...] + noise_ref[...] * lax.rsqrt(2000.0 * (prec_ref[...] + 0.1))
     weights = weight_matrix(noisy, cout, cin)
     w_ref[...] = weights
     total = jnp.zeros((cout, width), F32)
+    grads = [matmul(there, jnp.concatenate([g_ref[i, j] for j in range(nj)], axis=1)) for i in range(ni)]
+    g0_ref[...] = grads[0]
     for i in range(1, ni):
         preact = matmul(weights, cols_ref[i - 1])
-        grads = jnp.concatenate([g_ref[i, j] for j in range(nj)], axis=1).astype(F32)
-        act, pre = activate(preact, grads)
+        act, pre = activate(preact, grads[i])
+        act = matmul(back, act).astype(BF16)
         for j in range(nj):
             act_ref[i - 1, j] = act[:, j * half : (j + 1) * half]
         pre_ref[i - 1] = pre
         total = total + matmul_nt(pre, cols_ref[i - 1])
     total_ref[...] = total
-    first = depth // 3
-    part_ref[...] = matmul(weights[:, first:], col_ref[first:, :])
-
-
-def finish_kernel(halo_ref, act_rest_ref, pre_rest_ref, w_ref, part_ref, total_ref, col_in_ref, g_hbm,
-                  act_ref, pack_ref, rim_ref, dw_ref, col_ref, g_ref, sem):
+    tail = tail_rows(cin)
+    part_ref[...] = matmul(weights[:, :tail], col_ref[:tail, :])
+
+
+def finish_kernel(halo_ref, act_rest_ref, pre_rest_ref, w_ref, part_ref, total_ref, col_in_ref, pick_ref, g0_ref,
+                  act_ref, pack_ref, rim_ref, dw_ref, col_ref):
     ys, cin, zs = halo_ref.shape
     ni, nj, cout, half = act_ref.shape
-    first = len(TAPS) * cin // 3
-    copy = pltpu.make_async_copy(g_hbm.at[0], g_ref, sem)
-    copy.start()
-    picked = matmul(halo_ref[...].reshape(ys * cin, zs), pick_strided(zs))
-    picked = (picked * unless("space", 0)).astype(BF16)
-    place_plane(picked, -1, ys, cin, half, {0: col_ref})
-    preact = part_ref[...] + matmul(w_ref[:, :first], col_ref[...])
-    copy.wait()
-    grads = jnp.concatenate([g_ref[j] for j in range(nj)], axis=1).astype(F32)
-    act, pre = activate(preact, grads)
+    width = w_ref.shape[1]
+    depth = len(TAPS) * cin
+    tail = tail_rows(cin)
+    kept = 2 * depth // 3
+    picked = matmul(halo_ref[...].reshape(ys * cin, zs), pick_ref[...]).astype(BF16)
+    col_ref[: kept - tail, :] = col_in_ref[tail:kept, :]
+    col_ref[depth - tail :, :] = jnp.zeros((width - depth, nj * half), BF16)
+    place_plane(picked, -1, ys, cin, half, {0: col_ref}, tail)
+    preact = part_ref[...] + matmul(w_ref[:, tail:], col_ref[...])
+    act, pre = activate(preact, g0_ref[...])
+    ours = jnp.concatenate([matmul_nt(pre, col_in_ref[:tail, :]), matmul_nt(pre, col_ref[...])], axis=1)
+    dw_ref[...] = weight_rows(total_ref[...] + ours, cout, cin)
+    rim_ref[...] = pre
+    act = matmul(regroup(cout, LANES // cin, True), act).astype(BF16)
     for j in range(nj):
         act_ref[0, j] = act[:, j * half : (j + 1) * half]
     act_ref[1:] = act_rest_ref[...]
-    rim_ref[...] = pre
     pack_ref[:, : nj * half] = pre
     for i in range(1, ni):
         pack_ref[:, i * nj * half : (i + 1) * nj * half] = pre_rest_ref[i - 1]
     pack_ref[:, ni * nj * half :] = w_ref[...]
-    ours = jnp.concatenate([matmul_nt(pre, col_ref[...]), matmul_nt(pre, col_in_ref[first:, :])], axis=1)
-    dw_ref[...] = weight_rows(total_ref[...] + ours, cout, cin)
 
 
 def parity_taps(parity, shift):
@@ -301,7 +323,7 @@
         return lax.psum(block, ("dp", "space")).astype(F32)
     stride = n_space // 2
     while stride > 1:
-        other = swapped(block, 0, stride)
+        other = swapped(block, 0, 2 * stride - 1)
         block = (block.astype(F32) + other.astype(F32)).astype(BF16)
         stride //= 2
     both = swapped(block, 1, 1)
@@ -325,9 +347,18 @@
     noise = weight_noise.reshape(flat)
     width = pl.cdiv(len(TAPS) * cin, LANES) * LANES
 
-    below = passed_along(feats[xd - 1], {"space": 1})
+    plane = pl.pallas_call(
+        plane_kernel,
+        out_shape=jax.ShapeDtypeStruct(feats.shape[1:], BF16),
+        in_specs=[pl.BlockSpec(memory_space=pltpu.HBM)],
+        out_specs=pl.BlockSpec(memory_space=pltpu.VMEM),
+        scratch_shapes=[pltpu.SemaphoreType.DMA],
+        compiler_params=params(8),
+        name="plane",
+    )(pltpu.with_memory_space_constraint(feats, pltpu.HBM))
+    below = passed_along(plane, {"space": 1})
     shape = jax.ShapeDtypeStruct
-    act_rest, pre_rest, weights, part, total, col = pl.pallas_call(
+    act_rest, pre_rest, weights, part, total, col, pick, grads0 = pl.pallas_call(
         prepare_kernel,
         out_shape=(
             shape((ni - 1, nj, cout, half), BF16),
@@ -336,6 +367,8 @@
             shape((cout, nj * half), F32),
             shape((cout, width), F32),
             shape((width, nj * half), BF16),
+            shape((zs, 3 * half), BF16),
+            shape((cout, nj * half), F32),
         ),
         in_specs=[pl.BlockSpec(memory_space=pltpu.HBM)] * 5,
         scratch_shapes=[
@@ -359,15 +392,11 @@
             shape((cout, nj * half), BF16),
             shape(flat, BF16),
         ),
-        in_specs=[vmem] * 7 + [pl.BlockSpec(memory_space=pltpu.HBM)],
-        scratch_shapes=[
-            pltpu.VMEM((len(TAPS) * cin // 3, nj * half), BF16),
-            pltpu.VMEM(grads.shape[1:], BF16),
-            pltpu.SemaphoreType.DMA,
-        ],
+        in_specs=[vmem] * 9,
+        scratch_shapes=[pltpu.VMEM((width - tail_rows(cin), nj * half), BF16)],
         compiler_params=params(24),
         name="finish",
-    )(below, act_rest, pre_rest, weights, part, total, col, grads)
+    )(below, act_rest, pre_rest, weights, part, total, col, pick, grads0)
     pack = passed_along(pack, {"segment": -1})
     rim = passed_along(rim, {"segment": -1, "space": -1})
     act_in = passed_along(act, {"segment": 1})

time: 32.6 us -> 31.5 us (0.966)
  waiting for transfers between devices: 12.2 us -> 10.6 us
  starting transfers between devices: 10.3 us -> 11.5 us
  local copies, waits for them, and re-layouts: 0.92 us -> 0.01 us
    ppermute x4, waiting for transfers between devices: 8.42 us -> 6.86 us  [swapped(): return lax.ppermute(block, ('dp', 'space'), route)]
    ppermute x4, starting transfers between devices: 4.83 us -> 5.8 us  [swapped(): return lax.ppermute(block, ('dp', 'space'), route)]
    pallas_call x0 -> x1, Pallas kernels: none -> 0.91 us  [step(): pl.pallas_call(plane_kernel, out_shape=jax.ShapeDtypeStruct(feats.shape[1...]
    squeeze x1 -> x0, local copies, waits for them, and re-layouts: 0.9 us -> none  [step(): below = passed_along(feats[xd - 1], {'space': 1})]
    pallas_call x1, Pallas kernels: 1.17 us -> 0.74 us  [step(): pl.pallas_call(finish_kernel, out_shape=(shape((ni, nj, cout, half), BF16...]
  transfers between devices with their start and end apart: 8 -> 8, of which waited for: 6 -> 5; matrix products, arithmetic and copies ran while one was open for 3% -> 3% of each run, Pallas kernels for 10% -> 10%
where the time goes in v4:
time: 31.5 us; the launch traced here: 31.3 us
  starting transfers between devices  11.5 us (37%)
  waiting for transfers between devices  10.6 us (34%)
  Pallas kernels  7.6 us (24%)
  other arithmetic  0.93 us (3%)
  between operations  0.67 us (2%)
    ppermute x4, waiting for transfers between devices, swapped(): return lax.ppermute(block, ('dp', 'space'), route)  6.86 us
    ppermute x4, starting transfers between devices, swapped(): return lax.ppermute(block, ('dp', 'space'), route)  5.8 us
    ppermute x4, starting transfers between devices, passed_along(): return lax.ppermute(block, axes, route)  5.72 us
    ppermute x4, waiting for transfers between devices, passed_along(): return lax.ppermute(block, axes, route)  3.75 us
    pallas_call x1, Pallas kernels, step(): pl.pallas_call(prepare_kernel, out_shape=(shape((ni - 1, nj, cout, half),...  3.09 us
    pallas_call x1, Pallas kernels, step(): pl.pallas_call(input_kernel, out_shape=(shape((xd, ys, cin, zs), BF16), s...  2.85 us
    pallas_call x1, Pallas kernels, step(): pl.pallas_call(plane_kernel, out_shape=jax.ShapeDtypeStruct(feats.shape[1...  0.91 us
    add x1, other arithmetic, step(): prec_next = 0.75 * prec + 0.25 * scaled * scaled  0.89 us
  transfers between devices with their start and end apart: 8, of which 5 were waited for; matrix products, arithmetic and copies ran while one was open for 3% of the time, Pallas kernels for 10%

profile of v4, /device:TPU:0, one launch (start us, length us, event | category | flops | bytes accessed | tf_op | source)
XLA Modules:
  0.0 31.3 jit_solution(5839751361697137303)
XLA Ops:
  0.6 0.9 %plane.1 = bf16[6,32,256]{2,1,0:T(8,128)(2,1)S(1)} custom-call(bf16[6,6,32,256]{3,2,1,0:T(8,128)(2,1)} %bitcast.17), custom_call_target="tpu_custom_call" | custom-call | tf_op jit(solution)/shard_map/plane/pallas_call | solution.py:350
  1.6 3.1 %collective-permute-start = (bf16[6,32,256]{2,1,0:T(8,128)(2,1)S(1)}, bf16[6,32,256]{2,1,0:T(8,128)(2,1)S(1)}, u32[]{:S(2)}, u32[]{:S(2)}) collective-permute-start(bf16[6,32,256]{2,1,0:T(8,128)(2,1)S(1)} %plane.1), channel_id=1, source_target_pairs={{0,1},{1,2},{2,3},{3,0},{4,5},{5,6},{6,7},{7,4},{8,9},{9,10},{10,1... | collective-permute-start | bytes 294920 | tf_op jit(solution)/shard_map/ppermute | solution.py:28
  4.7 3.1 %prepare.1 = (bf16[2,3,64,128]{3,2,1,0:T(8,128)(2,1)S(1)}, bf16[2,64,384]{2,1,0:T(8,128)(2,1)S(1)}, bf16[64,896]{1,0:T(8,128)(2,1)S(1)}, f32[64,384]{1,0:T(8,128...) custom-call(bf16[6,6,32,256]{3,2,1,0:T(8,128)(2,1)} %bitcast.18, ...), custom_call_target="tpu_custom_call" | custom-call | tf_op jit(solution)/shard_map/prepare/pallas_call | solution.py:361
  7.8 0.8 %collective-permute-done.halo_ref = bf16[6,32,256]{2,1,0:T(8,128)(2,1)S(1)} collective-permute-done((bf16[6,32,256]{2,1,0:T(8,128)(2,1)S(1)}, bf16[6,32,256]{2,1,0:T(8,128)(2,1)S(1)}, u32[]{:S(2)}, u32[]{:S(2)}) %collective-permute-start) | collective-permute-done | bytes 98336 | tf_op jit(solution)/shard_map/ppermute | solution.py:28
  8.6 0.0 copy-start.1
  8.6 0.7 %finish.1 = (bf16[3,3,64,128]{3,2,1,0:T(8,128)(2,1)S(1)}, bf16[64,2048]{1,0:T(8,128)(2,1)S(1)}, bf16[64,384]{1,0:T(8,128)(2,1)S(1)}, bf16[432,128]{1,0:T(8,128)(2,1)S(1)}) custom-call(bf16[6,32,256]{2,1,0:T(8,128)(2,1)S(1)} %collective-permute-done.halo_ref, bf16[2,3,64,128]{3,2,1,0:T(8,128)(2,1)S(1)} %get-tuple-element.18.act_rest_ref, ...), custom_call_target="tpu_custom_call" | custom-call | tf_op jit(solution)/shard_map/finish/pallas_call | solution.py:387
  9.3 0.0 copy-start
  9.4 1.9 %collective-permute-start.4 = (bf16[432,128]{1,0:T(8,128)(2,1)S(1)}, bf16[432,128]{1,0:T(8,128)(2,1)S(1)}, u32[]{:S(2)}, u32[]{:S(2)}) collective-permute-start(bf16[432,128]{1,0:T(8,128)(2,1)S(1)} %get-tuple-element.31), channel_id=1, source_target_pairs={{0,3},{1,2},{2,1},{3,0},{16,19},{17,18},{18,17},{19,16},{4,7},{5,6... | collective-permute-start | bytes 331784 | tf_op jit(solution)/shard_map/ppermute | solution.py:317
  11.2 4.7 %collective-permute-done.4 = bf16[432,128]{1,0:T(8,128)(2,1)S(1)} collective-permute-done((bf16[432,128]{1,0:T(8,128)(2,1)S(1)}, bf16[432,128]{1,0:T(8,128)(2,1)S(1)}, u32[]{:S(2)}, u32[]{:S(2)}) %collective-permute-start.4) | collective-permute-done | bytes 110624 | tf_op jit(solution)/shard_map/ppermute | solution.py:317
  16.0 1.1 %collective-permute-start.7 = (bf16[432,128]{1,0:T(8,128)(2,1)S(1)}, bf16[432,128]{1,0:T(8,128)(2,1)S(1)}, u32[]{:S(2)}, u32[]{:S(2)}) collective-permute-start(bf16[432,128]{1,0:T(8,128)(2,1)S(1)} %add_convert_fusion), channel_id=1, source_target_pairs={{0,17},{1,16},{2,19},{3,18},{16,1},{17,0},{18,3},{19,2},{4,21},{5,... | collective-permute-start | bytes 331784 | tf_op jit(solution)/shard_map/ppermute | solution.py:317
  17.1 2.8 %collective-permute-start.6 = (bf16[432,128]{1,0:T(8,128)(2,1)S(1)}, bf16[432,128]{1,0:T(8,128)(2,1)S(1)}, u32[]{:S(2)}, u32[]{:S(2)}) collective-permute-start(bf16[432,128]{1,0:T(8,128)(2,1)S(1)} %add_convert_fusion), channel_id=1, source_target_pairs={{0,1},{1,0},{2,3},{3,2},{16,17},{17,16},{18,19},{19,18},{4,5},{5,4... | collective-permute-start | bytes 331784 | tf_op jit(solution)/shard_map/ppermute | solution.py:317
  19.9 0.0 collective-permute-start.5
  19.9 0.0 collective-permute-start.1
  19.9 2.6 %collective-permute-start.2 = (bf16[64,384]{1,0:T(8,128)(2,1)S(1)}, bf16[64,384]{1,0:T(8,128)(2,1)S(1)}, u32[]{:S(2)}, u32[]{:S(2)}) collective-permute-start(bf16[64,384]{1,0:T(8,128)(2,1)S(1)} %get-tuple-element.27), channel_id=1, source_target_pairs={{0,15},{1,12},{2,13},{3,14},{4,3},{5,0},{6,1},{7,2},{8,7},{9,4},{1... | collective-permute-start | bytes 147464 | tf_op jit(solution)/shard_map/ppermute | solution.py:28
  22.5 0.0 collective-permute-done.7
  22.5 0.0 collective-permute-start.3
  22.6 1.8 %collective-permute-done.6 = bf16[432,128]{1,0:T(8,128)(2,1)S(1)} collective-permute-done((bf16[432,128]{1,0:T(8,128)(2,1)S(1)}, bf16[432,128]{1,0:T(8,128)(2,1)S(1)}, u32[]{:S(2)}, u32[]{:S(2)}) %collective-permute-start.6) | collective-permute-done | bytes 110624 | tf_op jit(solution)/shard_map/ppermute | solution.py:317
  24.4 0.3 %collective-permute-done.5 = bf16[432,128]{1,0:T(8,128)(2,1)S(1)} collective-permute-done((bf16[432,128]{1,0:T(8,128)(2,1)S(1)}, bf16[432,128]{1,0:T(8,128)(2,1)S(1)}, u32[]{:S(2)}, u32[]{:S(2)}) %collective-permute-start.5) | collective-permute-done | bytes 110624 | tf_op jit(solution)/shard_map/ppermute | solution.py:317
  24.7 0.0 copy-done.1
  24.7 0.0 copy-done
  24.7 0.9 %multiply_add_fusion = (f32[432,128]{1,0:T(8,128)}, f32[432,128]{1,0:T(8,128)}) fusion(f32[432,128]{1,0:T(8,128)S(1)} %bitcast.22, bf16[432,128]{1,0:T(8,128)(2,1)S(1)} %collective-permute-done.7, bf16[432,128]{1,0:T(8,128)(2,1)S(1)} %collective-permute-done.6, bf16[432,128]{1,0:T(8,128)(2,1)S(1)} %collective-permute-done.5, ...), kind=kLoop, calls=%fused_computation.1 | loop fusion | flops 884736 | bytes 1327104 | tf_op jit(solution)/shard_map/add | solution.py:423
  25.6 0.0 collective-permute-done.2.rim_ref
  25.6 2.9 %collective-permute-done.3.act_ref = bf16[3,3,64,128]{3,2,1,0:T(8,128)(2,1)S(1)} collective-permute-done((bf16[3,3,64,128]{3,2,1,0:T(8,128)(2,1)S(1)}, bf16[3,3,64,128]{3,2,1,0:T(8,128)(2,1)S(1)}, u32[]{:S(2)}, u32[]{:S(2)}) %collective-permute-start.3) | collective-permute-done | bytes 147488 | tf_op jit(solution)/shard_map/ppermute | solution.py:28
  28.5 0.0 collective-permute-done.1.pack_ref
  28.5 2.9 %input_grad.1 = (bf16[6,6,32,256]{3,2,1,0:T(8,128)(2,1)}, bf16[3,3,64,128]{3,2,1,0:T(8,128)(2,1)}) custom-call(bf16[64,2048]{1,0:T(8,128)(2,1)S(1)} %collective-permute-done.1.pack_ref, bf16[64,384]{1,0:T(8,128)(2,1)S(1)} %collective-permute-done.2.rim_ref, bf16[3,3,64,128]{3,2,1,0:T(8,128)(2,1)S(1)} %collective-permute-done.3.act_ref), custom_call_target="tpu_custom_call" | custom-call | tf_op jit(solution)/shard_map/input_grad/pallas_call | solution.py:404
  (1 shorter events, 0.0 us)
Async XLA Ops:
  1.6 7.0 %collective-permute-start = (bf16[6,32,256]{2,1,0:T(8,128)(2,1)S(1)}, bf16[6,32,256]{2,1,0:T(8,128)(2,1)S(1)}, u32[]{:S(2)}, u32[]{:S(2)}) collective-permute-start(bf16[6,32,256]{2,1,0:T(8,128)(2,1)S(1)} %plane.1), channel_id=1, source_target_pairs={{0,1},{1,2},{2,3},{3,0},{4,5},{5,6},{6,7},{7,4},{8,9},{9,10},{10,1... | collective-permute-start | bytes 294920 | tf_op jit(solution)/shard_map/ppermute | solution.py:28
  8.6 16.1 %copy-start.1 = (f32[1,27,2048]{2,0,1:T(1,128)S(1)}, f32[1,27,2048]{2,0,1:T(1,128)}, u32[]{:S(2)}) copy-start(f32[1,27,2048]{2,0,1:T(1,128)} %param.9) | copy-start | bytes 663556
  9.3 15.3 %copy-start = (f32[1,27,2048]{2,0,1:T(1,128)S(1)}, f32[1,27,2048]{2,0,1:T(1,128)}, u32[]{:S(2)}) copy-start(f32[1,27,2048]{2,0,1:T(1,128)} %param.7) | copy-start | bytes 663556
  9.4 6.6 %collective-permute-start.4 = (bf16[432,128]{1,0:T(8,128)(2,1)S(1)}, bf16[432,128]{1,0:T(8,128)(2,1)S(1)}, u32[]{:S(2)}, u32[]{:S(2)}) collective-permute-start(bf16[432,128]{1,0:T(8,128)(2,1)S(1)} %get-tuple-element.31), channel_id=1, source_target_pairs={{0,3},{1,2},{2,1},{3,0},{16,19},{17,18},{18,17},{19,16},{4,7},{5,6... | collective-permute-start | bytes 331784 | tf_op jit(solution)/shard_map/ppermute | solution.py:317
  16.0 6.5 %collective-permute-start.7 = (bf16[432,128]{1,0:T(8,128)(2,1)S(1)}, bf16[432,128]{1,0:T(8,128)(2,1)S(1)}, u32[]{:S(2)}, u32[]{:S(2)}) collective-permute-start(bf16[432,128]{1,0:T(8,128)(2,1)S(1)} %add_convert_fusion), channel_id=1, source_target_pairs={{0,17},{1,16},{2,19},{3,18},{16,1},{17,0},{18,3},{19,2},{4,21},{5,... | collective-permute-start | bytes 331784 | tf_op jit(solution)/shard_map/ppermute | solution.py:317
  17.1 7.2 %collective-permute-start.6 = (bf16[432,128]{1,0:T(8,128)(2,1)S(1)}, bf16[432,128]{1,0:T(8,128)(2,1)S(1)}, u32[]{:S(2)}, u32[]{:S(2)}) collective-permute-start(bf16[432,128]{1,0:T(8,128)(2,1)S(1)} %add_convert_fusion), channel_id=1, source_target_pairs={{0,1},{1,0},{2,3},{3,2},{16,17},{17,16},{18,19},{19,18},{4,5},{5,4... | collective-permute-start | bytes 331784 | tf_op jit(solution)/shard_map/ppermute | solution.py:317
  19.9 4.7 %collective-permute-start.5 = (bf16[432,128]{1,0:T(8,128)(2,1)S(1)}, bf16[432,128]{1,0:T(8,128)(2,1)S(1)}, u32[]{:S(2)}, u32[]{:S(2)}) collective-permute-start(bf16[432,128]{1,0:T(8,128)(2,1)S(1)} %add_convert_fusion), channel_id=1, source_target_pairs={{0,16},{1,17},{2,18},{3,19},{16,0},{17,1},{18,2},{19,3},{4,20},{5,... | collective-permute-start | bytes 331784 | tf_op jit(solution)/shard_map/ppermute | solution.py:317
  19.9 8.6 %collective-permute-start.1 = (bf16[64,2048]{1,0:T(8,128)(2,1)S(1)}, bf16[64,2048]{1,0:T(8,128)(2,1)S(1)}, u32[]{:S(2)}, u32[]{:S(2)}) collective-permute-start(bf16[64,2048]{1,0:T(8,128)(2,1)S(1)} %get-tuple-element.26), channel_id=1, source_target_pairs={{0,12},{4,0},{8,4},{12,8},{1,13},{5,1},{9,5},{13,9},{2,14},{6,2},{... | collective-permute-start | bytes 786440 | tf_op jit(solution)/shard_map/ppermute | solution.py:28
  19.9 5.6 %collective-permute-start.2 = (bf16[64,384]{1,0:T(8,128)(2,1)S(1)}, bf16[64,384]{1,0:T(8,128)(2,1)S(1)}, u32[]{:S(2)}, u32[]{:S(2)}) collective-permute-start(bf16[64,384]{1,0:T(8,128)(2,1)S(1)} %get-tuple-element.27), channel_id=1, source_target_pairs={{0,15},{1,12},{2,13},{3,14},{4,3},{5,0},{6,1},{7,2},{8,7},{9,4},{1... | collective-permute-start | bytes 147464 | tf_op jit(solution)/shard_map/ppermute | solution.py:28
  22.5 5.9 %collective-permute-start.3 = (bf16[3,3,64,128]{3,2,1,0:T(8,128)(2,1)S(1)}, bf16[3,3,64,128]{3,2,1,0:T(8,128)(2,1)S(1)}, u32[]{:S(2)}, u32[]{:S(2)}) collective-permute-start(bf16[3,3,64,128]{3,2,1,0:T(8,128)(2,1)S(1)} %get-tuple-element.28), channel_id=1, source_target_pairs={{0,4},{4,8},{8,12},{12,0},{1,5},{5,9},{9,13},{13,1},{2,6},{6,10},{... | collective-permute-start | bytes 442376 | tf_op jit(solution)/shard_map/ppermute | solution.py:28

commit v5 on v4

--- a/solution.py
+++ b/solution.py
@@ -176,12 +176,11 @@
     pick = pick_strided(zs)
     pick_ref[...] = pick
     there, back = regroup(cout, LANES // cin), regroup(cout, LANES // cin, True)
-    for x in range(0, xd, 2):
+    for x in range(xd):
         order[x].wait()
-        order[x + 1].wait()
-        picked = matmul(x_ref[x : x + 2].reshape(2 * ys * cin, zs), pick).astype(BF16)
-        place_plane(picked[: ys * cin], x, ys, cin, half, targets)
-        place_plane(picked[ys * cin :], x + 1, ys, cin, half, targets)
+    every = matmul(x_ref[...].reshape(xd * ys * cin, zs), pick).astype(BF16)
+    for x in range(xd):
+        place_plane(every[x * ys * cin : (x + 1) * ys * cin], x, ys, cin, half, targets)
     for copy in rest:
         copy.wait()
     noisy = mean_ref[...] + noise_ref[...] * lax.rsqrt(2000.0 * (prec_ref[...] + 0.1))

time: 31.5 us -> 31.7 us (level)
  transfers between devices with their start and end apart: 8 -> 8, of which waited for: 5 -> 5; matrix products, arithmetic and copies ran while one was open for 3% -> 3% of each run, Pallas kernels for 10% -> 9%
where the time goes in v5:
time: 31.7 us; the launch traced here: 31.5 us
  starting transfers between devices  11.5 us (36%)
  waiting for transfers between devices  10.9 us (34%)
  Pallas kernels  7.48 us (24%)
  other arithmetic  0.93 us (3%)
  between operations  0.67 us (2%)
    ppermute x4, waiting for transfers between devices, swapped(): return lax.ppermute(block, ('dp', 'space'), route)  6.86 us
    ppermute x4, starting transfers between devices, swapped(): return lax.ppermute(block, ('dp', 'space'), route)  5.8 us
    ppermute x4, starting transfers between devices, passed_along(): return lax.ppermute(block, axes, route)  5.72 us
    ppermute x4, waiting for transfers between devices, passed_along(): return lax.ppermute(block, axes, route)  4.01 us
    pallas_call x1, Pallas kernels, step(): pl.pallas_call(prepare_kernel, out_shape=(shape((ni - 1, nj, cout, half),...  2.97 us
    pallas_call x1, Pallas kernels, step(): pl.pallas_call(input_kernel, out_shape=(shape((xd, ys, cin, zs), BF16), s...  2.85 us
    pallas_call x1, Pallas kernels, step(): pl.pallas_call(plane_kernel, out_shape=jax.ShapeDtypeStruct(feats.shape[1...  0.91 us
    add x1, other arithmetic, step(): prec_next = 0.75 * prec + 0.25 * scaled * scaled  0.89 us
  transfers between devices with their start and end apart: 8, of which 5 were waited for; matrix products, arithmetic and copies ran while one was open for 3% of the time, Pallas kernels for 9%

profile of v5, /device:TPU:0, one launch (start us, length us, event | category | flops | bytes accessed | tf_op | source)
XLA Modules:
  0.0 31.5 jit_solution(15377931467518530537)
XLA Ops:
  0.6 0.9 %plane.1 = bf16[6,32,256]{2,1,0:T(8,128)(2,1)S(1)} custom-call(bf16[6,6,32,256]{3,2,1,0:T(8,128)(2,1)} %bitcast.17), custom_call_target="tpu_custom_call" | custom-call | tf_op jit(solution)/shard_map/plane/pallas_call | solution.py:349
  1.6 3.1 %collective-permute-start = (bf16[6,32,256]{2,1,0:T(8,128)(2,1)S(1)}, bf16[6,32,256]{2,1,0:T(8,128)(2,1)S(1)}, u32[]{:S(2)}, u32[]{:S(2)}) collective-permute-start(bf16[6,32,256]{2,1,0:T(8,128)(2,1)S(1)} %plane.1), channel_id=1, source_target_pairs={{0,1},{1,2},{2,3},{3,0},{4,5},{5,6},{6,7},{7,4},{8,9},{9,10},{10,1... | collective-permute-start | bytes 294920 | tf_op jit(solution)/shard_map/ppermute | solution.py:28
  4.7 3.0 %prepare.1 = (bf16[2,3,64,128]{3,2,1,0:T(8,128)(2,1)S(1)}, bf16[2,64,384]{2,1,0:T(8,128)(2,1)S(1)}, bf16[64,896]{1,0:T(8,128)(2,1)S(1)}, f32[64,384]{1,0:T(8,128...) custom-call(bf16[6,6,32,256]{3,2,1,0:T(8,128)(2,1)} %bitcast.18, ...), custom_call_target="tpu_custom_call" | custom-call | tf_op jit(solution)/shard_map/prepare/pallas_call | solution.py:360
  7.6 1.0 %collective-permute-done.halo_ref = bf16[6,32,256]{2,1,0:T(8,128)(2,1)S(1)} collective-permute-done((bf16[6,32,256]{2,1,0:T(8,128)(2,1)S(1)}, bf16[6,32,256]{2,1,0:T(8,128)(2,1)S(1)}, u32[]{:S(2)}, u32[]{:S(2)}) %collective-permute-start) | collective-permute-done | bytes 98336 | tf_op jit(solution)/shard_map/ppermute | solution.py:28
  8.6 0.0 copy-start.1
  8.6 0.7 %finish.1 = (bf16[3,3,64,128]{3,2,1,0:T(8,128)(2,1)S(1)}, bf16[64,2048]{1,0:T(8,128)(2,1)S(1)}, bf16[64,384]{1,0:T(8,128)(2,1)S(1)}, bf16[432,128]{1,0:T(8,128)(2,1)S(1)}) custom-call(bf16[6,32,256]{2,1,0:T(8,128)(2,1)S(1)} %collective-permute-done.halo_ref, bf16[2,3,64,128]{3,2,1,0:T(8,128)(2,1)S(1)} %get-tuple-element.18.act_rest_ref, ...), custom_call_target="tpu_custom_call" | custom-call | tf_op jit(solution)/shard_map/finish/pallas_call | solution.py:386
  9.3 0.0 copy-start
  9.4 1.9 %collective-permute-start.4 = (bf16[432,128]{1,0:T(8,128)(2,1)S(1)}, bf16[432,128]{1,0:T(8,128)(2,1)S(1)}, u32[]{:S(2)}, u32[]{:S(2)}) collective-permute-start(bf16[432,128]{1,0:T(8,128)(2,1)S(1)} %get-tuple-element.31), channel_id=1, source_target_pairs={{0,3},{1,2},{2,1},{3,0},{16,19},{17,18},{18,17},{19,16},{4,7},{5,6... | collective-permute-start | bytes 331784 | tf_op jit(solution)/shard_map/ppermute | solution.py:316
  11.2 4.7 %collective-permute-done.4 = bf16[432,128]{1,0:T(8,128)(2,1)S(1)} collective-permute-done((bf16[432,128]{1,0:T(8,128)(2,1)S(1)}, bf16[432,128]{1,0:T(8,128)(2,1)S(1)}, u32[]{:S(2)}, u32[]{:S(2)}) %collective-permute-start.4) | collective-permute-done | bytes 110624 | tf_op jit(solution)/shard_map/ppermute | solution.py:316
  16.0 1.1 %collective-permute-start.7 = (bf16[432,128]{1,0:T(8,128)(2,1)S(1)}, bf16[432,128]{1,0:T(8,128)(2,1)S(1)}, u32[]{:S(2)}, u32[]{:S(2)}) collective-permute-start(bf16[432,128]{1,0:T(8,128)(2,1)S(1)} %add_convert_fusion), channel_id=1, source_target_pairs={{0,17},{1,16},{2,19},{3,18},{16,1},{17,0},{18,3},{19,2},{4,21},{5,... | collective-permute-start | bytes 331784 | tf_op jit(solution)/shard_map/ppermute | solution.py:316
  17.1 2.9 %collective-permute-start.6 = (bf16[432,128]{1,0:T(8,128)(2,1)S(1)}, bf16[432,128]{1,0:T(8,128)(2,1)S(1)}, u32[]{:S(2)}, u32[]{:S(2)}) collective-permute-start(bf16[432,128]{1,0:T(8,128)(2,1)S(1)} %add_convert_fusion), channel_id=1, source_target_pairs={{0,1},{1,0},{2,3},{3,2},{16,17},{17,16},{18,19},{19,18},{4,5},{5,4... | collective-permute-start | bytes 331784 | tf_op jit(solution)/shard_map/ppermute | solution.py:316
  19.9 0.0 collective-permute-start.5
  19.9 0.0 collective-permute-start.1
  19.9 2.6 %collective-permute-start.2 = (bf16[64,384]{1,0:T(8,128)(2,1)S(1)}, bf16[64,384]{1,0:T(8,128)(2,1)S(1)}, u32[]{:S(2)}, u32[]{:S(2)}) collective-permute-start(bf16[64,384]{1,0:T(8,128)(2,1)S(1)} %get-tuple-element.27), channel_id=1, source_target_pairs={{0,15},{1,12},{2,13},{3,14},{4,3},{5,0},{6,1},{7,2},{8,7},{9,4},{1... | collective-permute-start | bytes 147464 | tf_op jit(solution)/shard_map/ppermute | solution.py:28
  22.5 0.0 collective-permute-done.7
  22.5 0.0 collective-permute-start.3
  22.6 1.8 %collective-permute-done.6 = bf16[432,128]{1,0:T(8,128)(2,1)S(1)} collective-permute-done((bf16[432,128]{1,0:T(8,128)(2,1)S(1)}, bf16[432,128]{1,0:T(8,128)(2,1)S(1)}, u32[]{:S(2)}, u32[]{:S(2)}) %collective-permute-start.6) | collective-permute-done | bytes 110624 | tf_op jit(solution)/shard_map/ppermute | solution.py:316
  24.4 0.3 collective-permute-done.5
  24.7 0.0 copy-done.1
  24.7 0.0 copy-done
  24.7 0.9 %multiply_add_fusion = (f32[432,128]{1,0:T(8,128)}, f32[432,128]{1,0:T(8,128)}) fusion(f32[432,128]{1,0:T(8,128)S(1)} %bitcast.22, bf16[432,128]{1,0:T(8,128)(2,1)S(1)} %collective-permute-done.7, bf16[432,128]{1,0:T(8,128)(2,1)S(1)} %collective-permute-done.6, bf16[432,128]{1,0:T(8,128)(2,1)S(1)} %collective-permute-done.5, ...), kind=kLoop, calls=%fused_computation.1 | loop fusion | flops 884736 | bytes 1327104 | tf_op jit(solution)/shard_map/add | solution.py:422
  25.6 0.0 collective-permute-done.2.rim_ref
  25.6 3.0 %collective-permute-done.3.act_ref = bf16[3,3,64,128]{3,2,1,0:T(8,128)(2,1)S(1)} collective-permute-done((bf16[3,3,64,128]{3,2,1,0:T(8,128)(2,1)S(1)}, bf16[3,3,64,128]{3,2,1,0:T(8,128)(2,1)S(1)}, u32[]{:S(2)}, u32[]{:S(2)}) %collective-permute-start.3) | collective-permute-done | bytes 147488 | tf_op jit(solution)/shard_map/ppermute | solution.py:28
  28.6 0.0 collective-permute-done.1.pack_ref
  28.6 2.9 %input_grad.1 = (bf16[6,6,32,256]{3,2,1,0:T(8,128)(2,1)}, bf16[3,3,64,128]{3,2,1,0:T(8,128)(2,1)}) custom-call(bf16[64,2048]{1,0:T(8,128)(2,1)S(1)} %collective-permute-done.1.pack_ref, bf16[64,384]{1,0:T(8,128)(2,1)S(1)} %collective-permute-done.2.rim_ref, bf16[3,3,64,128]{3,2,1,0:T(8,128)(2,1)S(1)} %collective-permute-done.3.act_ref), custom_call_target="tpu_custom_call" | custom-call | tf_op jit(solution)/shard_map/input_grad/pallas_call | solution.py:403
  (1 shorter events, 0.0 us)
Async XLA Ops:
  1.6 7.0 %collective-permute-start = (bf16[6,32,256]{2,1,0:T(8,128)(2,1)S(1)}, bf16[6,32,256]{2,1,0:T(8,128)(2,1)S(1)}, u32[]{:S(2)}, u32[]{:S(2)}) collective-permute-start(bf16[6,32,256]{2,1,0:T(8,128)(2,1)S(1)} %plane.1), channel_id=1, source_target_pairs={{0,1},{1,2},{2,3},{3,0},{4,5},{5,6},{6,7},{7,4},{8,9},{9,10},{10,1... | collective-permute-start | bytes 294920 | tf_op jit(solution)/shard_map/ppermute | solution.py:28
  8.6 16.1 %copy-start.1 = (f32[1,27,2048]{2,0,1:T(1,128)S(1)}, f32[1,27,2048]{2,0,1:T(1,128)}, u32[]{:S(2)}) copy-start(f32[1,27,2048]{2,0,1:T(1,128)} %param.9) | copy-start | bytes 663556
  9.3 15.3 %copy-start = (f32[1,27,2048]{2,0,1:T(1,128)S(1)}, f32[1,27,2048]{2,0,1:T(1,128)}, u32[]{:S(2)}) copy-start(f32[1,27,2048]{2,0,1:T(1,128)} %param.7) | copy-start | bytes 663556
  9.4 6.6 %collective-permute-start.4 = (bf16[432,128]{1,0:T(8,128)(2,1)S(1)}, bf16[432,128]{1,0:T(8,128)(2,1)S(1)}, u32[]{:S(2)}, u32[]{:S(2)}) collective-permute-start(bf16[432,128]{1,0:T(8,128)(2,1)S(1)} %get-tuple-element.31), channel_id=1, source_target_pairs={{0,3},{1,2},{2,1},{3,0},{16,19},{17,18},{18,17},{19,16},{4,7},{5,6... | collective-permute-start | bytes 331784 | tf_op jit(solution)/shard_map/ppermute | solution.py:316
  16.0 6.5 %collective-permute-start.7 = (bf16[432,128]{1,0:T(8,128)(2,1)S(1)}, bf16[432,128]{1,0:T(8,128)(2,1)S(1)}, u32[]{:S(2)}, u32[]{:S(2)}) collective-permute-start(bf16[432,128]{1,0:T(8,128)(2,1)S(1)} %add_convert_fusion), channel_id=1, source_target_pairs={{0,17},{1,16},{2,19},{3,18},{16,1},{17,0},{18,3},{19,2},{4,21},{5,... | collective-permute-start | bytes 331784 | tf_op jit(solution)/shard_map/ppermute | solution.py:316
  17.1 7.3 %collective-permute-start.6 = (bf16[432,128]{1,0:T(8,128)(2,1)S(1)}, bf16[432,128]{1,0:T(8,128)(2,1)S(1)}, u32[]{:S(2)}, u32[]{:S(2)}) collective-permute-start(bf16[432,128]{1,0:T(8,128)(2,1)S(1)} %add_convert_fusion), channel_id=1, source_target_pairs={{0,1},{1,0},{2,3},{3,2},{16,17},{17,16},{18,19},{19,18},{4,5},{5,4... | collective-permute-start | bytes 331784 | tf_op jit(solution)/shard_map/ppermute | solution.py:316
  19.9 4.7 %collective-permute-start.5 = (bf16[432,128]{1,0:T(8,128)(2,1)S(1)}, bf16[432,128]{1,0:T(8,128)(2,1)S(1)}, u32[]{:S(2)}, u32[]{:S(2)}) collective-permute-start(bf16[432,128]{1,0:T(8,128)(2,1)S(1)} %add_convert_fusion), channel_id=1, source_target_pairs={{0,16},{1,17},{2,18},{3,19},{16,0},{17,1},{18,2},{19,3},{4,20},{5,... | collective-permute-start | bytes 331784 | tf_op jit(solution)/shard_map/ppermute | solution.py:316
  19.9 8.7 %collective-permute-start.1 = (bf16[64,2048]{1,0:T(8,128)(2,1)S(1)}, bf16[64,2048]{1,0:T(8,128)(2,1)S(1)}, u32[]{:S(2)}, u32[]{:S(2)}) collective-permute-start(bf16[64,2048]{1,0:T(8,128)(2,1)S(1)} %get-tuple-element.26), channel_id=1, source_target_pairs={{0,12},{4,0},{8,4},{12,8},{1,13},{5,1},{9,5},{13,9},{2,14},{6,2},{... | collective-permute-start | bytes 786440 | tf_op jit(solution)/shard_map/ppermute | solution.py:28
  19.9 5.6 %collective-permute-start.2 = (bf16[64,384]{1,0:T(8,128)(2,1)S(1)}, bf16[64,384]{1,0:T(8,128)(2,1)S(1)}, u32[]{:S(2)}, u32[]{:S(2)}) collective-permute-start(bf16[64,384]{1,0:T(8,128)(2,1)S(1)} %get-tuple-element.27), channel_id=1, source_target_pairs={{0,15},{1,12},{2,13},{3,14},{4,3},{5,0},{6,1},{7,2},{8,7},{9,4},{1... | collective-permute-start | bytes 147464 | tf_op jit(solution)/shard_map/ppermute | solution.py:28
  22.5 6.1 %collective-permute-start.3 = (bf16[3,3,64,128]{3,2,1,0:T(8,128)(2,1)S(1)}, bf16[3,3,64,128]{3,2,1,0:T(8,128)(2,1)S(1)}, u32[]{:S(2)}, u32[]{:S(2)}) collective-permute-start(bf16[3,3,64,128]{3,2,1,0:T(8,128)(2,1)S(1)} %get-tuple-element.28), channel_id=1, source_target_pairs={{0,4},{4,8},{8,12},{12,0},{1,5},{5,9},{9,13},{13,1},{2,6},{6,10},{... | collective-permute-start | bytes 442376 | tf_op jit(solution)/shard_map/ppermute | solution.py:28
